TPU v7x, 32 devices: a whole 2x2x4 slice. The times are simulated.
32 devices in a mesh: proc: 8 (over z, y), loss: 2 (over x), vars: 2 (over core).
Axes of the slice: x: 2, y: 2, z: 4, core: 2. Of those that a mesh axis runs over, the one named last changes fastest.
Arguments:
- tokens: bfloat16 [16, 360, 1536], P('proc'), may hold values from -6 to 6
- shift: int32 [1], replicated, may hold values from 0 to 11
- w_qkv: bfloat16 [1536, 3, 16, 96], P(None, None, ('loss', 'vars')), may hold values from -0.15625 to 0.15625
- w_proj: bfloat16 [16, 96, 1536], replicated, may hold values from -0.15625 to 0.15625
- ln_gain: float32 [1536], replicated, may hold values from 0.1 to 1.9
- w_dec: bfloat16 [64, 4, 4, 1536], P(('loss', 'vars')), may hold values from -0.15625 to 0.15625
- prediction: bfloat16 [64, 64, 1440], P(('loss', 'vars'), 'proc'), may hold values from -6 to 6
- target: float32 [64, 64, 1440], P(('loss', 'vars'), 'proc'), may hold values from -12 to 12
- legendre: float32 [128, 64, 384], P('proc'), may hold values from -0.75 to 0.75
Outputs:
- amse: float32 [64], P(('loss', 'vars'))
- field_grad: float32 [64, 64, 1440], P(('loss', 'vars'), 'proc')
- input_grad: bfloat16 [16, 360, 1536], P('proc', None, ('loss', 'vars'))
Inputs may be any that keep to these rules, and one draw needn't show every extreme that they name: `shift`: the offset is the same for all tokens.
All inputs are finite; a program needn't handle non-finite values.
Results may differ from a plain program's by a relative error of at most 0.012.
Values may be sent and summed in bfloat16 or wider, within the bound.
A program may use at most 128 MiB of HBM per device.

v0:
```python
import functools
import math

import jax
import jax.numpy as jnp
import numpy as np
from jax import lax
from jax.experimental import pallas as pl
from jax.experimental.pallas import tpu as pltpu
from jax.sharding import PartitionSpec as P

HEAD = 96
VARS = 64
LON = 1440
LDEG = 384
WR = 2
WC = 12

EPSILON = 1e-06
NORM_EPSILON = 1e-05
HIGHEST = lax.Precision.HIGHEST
MESH = pl.DeviceIdType.MESH
F32 = jnp.float32
BF16 = jnp.bfloat16
VMEM = pl.BlockSpec(memory_space=pltpu.VMEM)
NT = (((1,), (1,)), ((), ()))


def fourier_basis(mode_count):
    column = np.arange(LON, dtype=np.int64)
    wavenumber = np.arange(mode_count, dtype=np.int64)
    phase = (column[:, None] * wavenumber[None, :] % LON) * (2.0 * math.pi / LON)
    return np.stack([np.cos(phase), -np.sin(phase)]) / math.sqrt(LON)


def amse_terms(power_pred, power_true, crossed):
    amp_pred = jnp.sqrt(power_pred + EPSILON)
    amp_true = jnp.sqrt(power_true + EPSILON)
    return (amp_pred - amp_true) ** 2 + 2.0 * jnp.maximum(power_pred, power_true) * (
        1.0 - crossed / (amp_pred * amp_true)
    )


def place(axis, index, sizes):
    proc, loss, var = (lax.axis_index(name) for name in ("proc", "loss", "vars"))
    if axis == "proc":
        return (index, loss, var)
    if axis == "loss":
        return (proc, index, var)
    if axis == "vars":
        return (proc, loss, index)
    return (proc, index // sizes["vars"], lax.rem(index, sizes["vars"]))


def rank(axis, sizes):
    if axis == "group":
        return lax.axis_index("loss") * sizes["vars"] + lax.axis_index("vars")
    return lax.axis_index(axis)


def greet(pairs):
    barrier = pltpu.get_barrier_semaphore()
    for device in pairs:
        pl.semaphore_signal(barrier, inc=1, device_id=device, device_id_type=MESH)
    pl.semaphore_wait(barrier, len(pairs))


def exchange_kernel(axis, count, sizes, spread, x_ref, out_ref, send, recv, own):
    me = rank(axis, sizes)
    peers = [lax.rem(me + k, count) for k in range(1, count)]
    greet([place(axis, peer, sizes) for peer in peers])
    copies = []
    for k, peer in enumerate(peers):
        copies.append(
            pltpu.make_async_remote_copy(
                src_ref=x_ref if spread else x_ref.at[peer],
                dst_ref=out_ref.at[me],
                send_sem=send.at[k],
                recv_sem=recv.at[k],
                device_id=place(axis, peer, sizes),
                device_id_type=MESH,
            )
        )
        copies[-1].start()
    local = pltpu.make_async_copy(x_ref if spread else x_ref.at[me], out_ref.at[me], own)
    local.start()
    local.wait()
    for copy in copies:
        copy.wait()


def exchange(x, axis, sizes, collective_id, spread=False):
    count = sizes["loss"] * sizes["vars"] if axis == "group" else sizes[axis]
    shape = (count,) + x.shape if spread else x.shape
    return pl.pallas_call(
        functools.partial(exchange_kernel, axis, count, sizes, spread),
        out_shape=jax.ShapeDtypeStruct(shape, x.dtype),
        in_specs=[VMEM],
        out_specs=VMEM,
        scratch_shapes=[
            pltpu.SemaphoreType.DMA((count - 1,)),
            pltpu.SemaphoreType.DMA((count - 1,)),
            pltpu.SemaphoreType.DMA,
        ],
        compiler_params=pltpu.CompilerParams(
            collective_id=collective_id, has_side_effects=True
        ),
        name="exchange_%d" % collective_id,
    )(x)


def total_kernel(count, sizes, x_ref, out_ref, parts, acc, send, recv, send2, recv2, own):
    me = rank("proc", sizes)
    peers = [lax.rem(me + k, count) for k in range(1, count)]
    greet([place("proc", peer, sizes) for peer in peers])

    def copy(src, dst, sems, k, peer):
        made = pltpu.make_async_remote_copy(
            src_ref=src,
            dst_ref=dst,
            send_sem=sems[0].at[k],
            recv_sem=sems[1].at[k],
            device_id=place("proc", peer, sizes),
            device_id_type=MESH,
        )
        made.start()
        return made

    first = [copy(x_ref.at[peer], parts.at[k], (send, recv), k, peer) for k, peer in enumerate(peers)]
    for made in first:
        made.wait()
    value = x_ref[me]
    for k in range(count - 1):
        value = value + parts[k]
    acc[...] = value
    second = [copy(acc, out_ref.at[me], (send2, recv2), k, peer) for k, peer in enumerate(peers)]
    local = pltpu.make_async_copy(acc, out_ref.at[me], own)
    local.start()
    local.wait()
    for made in second:
        made.wait()


def proc_total(x, sizes, collective_id):
    count = sizes["proc"]
    sems = [pltpu.SemaphoreType.DMA((count - 1,)) for _ in range(4)]
    return pl.pallas_call(
        functools.partial(total_kernel, count, sizes),
        out_shape=jax.ShapeDtypeStruct(x.shape, x.dtype),
        in_specs=[VMEM],
        out_specs=VMEM,
        scratch_shapes=[
            pltpu.VMEM((count - 1,) + x.shape[1:], x.dtype),
            pltpu.VMEM(x.shape[1:], x.dtype),
        ]
        + sems
        + [pltpu.SemaphoreType.DMA],
        compiler_params=pltpu.CompilerParams(
            collective_id=collective_id, has_side_effects=True
        ),
        name="proc_total",
    )(x)


def scatter_kernel(blocks, sizes, p_ref, kept_ref, out_ref, got, mid, far, s1, r1, s2, r2):
    loss_count, var_count = sizes["loss"], sizes["vars"]
    loss, var = lax.axis_index("loss"), lax.axis_index("vars")
    near = [lax.rem(var + k, var_count) for k in range(1, var_count)]
    away = [lax.rem(loss + k, loss_count) for k in range(1, loss_count)]
    greet(
        [place("vars", peer, sizes) for peer in near]
        + [place("loss", peer, sizes) for peer in away]
    )
    first, second = [], []
    for b in range(blocks):
        row = []
        for k, peer in enumerate(near):
            row.append(
                pltpu.make_async_remote_copy(
                    src_ref=p_ref.at[b, peer],
                    dst_ref=got.at[b, k],
                    send_sem=s1.at[b, k],
                    recv_sem=r1.at[b, k],
                    device_id=place("vars", peer, sizes),
                    device_id_type=MESH,
                )
            )
            row[-1].start()
        first.append(row)
    for b in range(blocks):
        for made in first[b]:
            made.wait()
        for j in range(loss_count):
            value = p_ref[b, var, j].astype(F32)
            for k in range(var_count - 1):
                value = value + got[b, k, j].astype(F32)
            mid[b, j] = value.astype(BF16)
        row = []
        for k, peer in enumerate(away):
            row.append(
                pltpu.make_async_remote_copy(
                    src_ref=mid.at[b, peer],
                    dst_ref=far.at[b, k],
                    send_sem=s2.at[b, k],
                    recv_sem=r2.at[b, k],
                    device_id=place("loss", peer, sizes),
                    device_id_type=MESH,
                )
            )
            row[-1].start()
        second.append(row)
    for b in range(blocks):
        value = kept_ref[b] + mid[b, loss].astype(F32)
        for made in second[b]:
            made.wait()
        for k in range(loss_count - 1):
            value = value + far[b, k].astype(F32)
        out_ref[b] = value.astype(BF16)


def reduce_group(parts, kept, sizes, collective_id):
    blocks, var_count, loss_count, rows, width = parts.shape
    return pl.pallas_call(
        functools.partial(scatter_kernel, blocks, sizes),
        out_shape=jax.ShapeDtypeStruct(kept.shape, BF16),
        in_specs=[VMEM, VMEM],
        out_specs=VMEM,
        scratch_shapes=[
            pltpu.VMEM((blocks, var_count - 1, loss_count, rows, width), BF16),
            pltpu.VMEM((blocks, loss_count, rows, width), BF16),
            pltpu.VMEM((blocks, loss_count - 1, rows, width), BF16),
            pltpu.SemaphoreType.DMA((blocks, var_count - 1)),
            pltpu.SemaphoreType.DMA((blocks, var_count - 1)),
            pltpu.SemaphoreType.DMA((blocks, loss_count - 1)),
            pltpu.SemaphoreType.DMA((blocks, loss_count - 1)),
        ],
        compiler_params=pltpu.CompilerParams(
            collective_id=collective_id, has_side_effects=True
        ),
        name="reduce_group",
    )(parts, kept)


def harmonics_kernel(modes, var_count, spectra_ref, legendre_ref, harm_ref, power_ref):
    half = 2 * var_count
    sums = [jnp.zeros((half, LDEG), F32) for _ in range(3)]
    for m in range(modes):
        harm = jnp.dot(
            spectra_ref[m], legendre_ref[m], precision=HIGHEST, preferred_element_type=F32
        )
        harm_ref[m] = harm
        pred, true = harm[:half], harm[half:]
        sums = [sums[0] + pred * pred, sums[1] + true * true, sums[2] + pred * true]
    for i in range(3):
        power_ref[i] = sums[i][:var_count] + sums[i][var_count:]


def harmonics(spectra, legendre):
    modes, rows, _ = spectra.shape
    var_count = rows // 4
    return pl.pallas_call(
        functools.partial(harmonics_kernel, modes, var_count),
        out_shape=(
            jax.ShapeDtypeStruct((modes, rows, LDEG), F32),
            jax.ShapeDtypeStruct((3, var_count, LDEG), F32),
        ),
        in_specs=[VMEM, VMEM],
        out_specs=(VMEM, VMEM),
        name="harmonics",
    )(spectra, legendre)


def spectra_grad_kernel(modes, pack, procs, var_count, harm_ref, legendre_ref, gp_ref, gc_ref, out_ref):
    half = 2 * var_count
    gp = jnp.concatenate([gp_ref[...], gp_ref[...]], axis=0) * 2.0
    gc = jnp.concatenate([gc_ref[...], gc_ref[...]], axis=0)
    for hi in range(modes // pack):
        columns = []
        for lo in range(pack):
            m = hi * pack + lo
            harm = harm_ref[m]
            grad = gp * harm[:half] + gc * harm[half:]
            columns.append(
                lax.dot_general(
                    legendre_ref[m], grad, NT, precision=HIGHEST, preferred_element_type=F32
                )
            )
        block = jnp.concatenate(columns, axis=1)
        out_ref[:, hi] = block.reshape(procs, block.shape[0] // procs, block.shape[1])


def spectra_grad(harm, legendre, gp, gc, procs):
    modes, rows, _ = harm.shape
    lats = legendre.shape[1]
    var_count = rows // 4
    pack = min(modes, max(1, 128 // (2 * var_count)))
    return pl.pallas_call(
        functools.partial(spectra_grad_kernel, modes, pack, procs, var_count),
        out_shape=jax.ShapeDtypeStruct(
            (procs, modes // pack, lats // procs, pack * 2 * var_count), F32
        ),
        in_specs=[VMEM] * 4,
        out_specs=VMEM,
        name="spectra_grad",
    )(harm, legendre, gp, gc), pack


def attention_kernel(
    heads, cols, groups, f_ref, coeff_ref, mix_ref, proj_ref, tok_ref, gain_ref, w_ref, part_ref, kept_ref
):
    loss_count, var_count = groups
    rows = WR * cols
    pieces = []
    for o in range(4):
        y = jnp.dot(f_ref[o], coeff_ref[0], preferred_element_type=F32)
        half = y.shape[1] // WR
        pieces.append(
            jnp.concatenate([y[:, r * half : (r + 1) * half] for r in range(WR)], axis=0).astype(BF16)
        )
    tiles = jnp.concatenate(pieces, axis=1)
    mixed = jnp.dot(tiles, mix_ref[...], preferred_element_type=F32)
    width = heads * HEAD
    grad_out = mixed[:, :width].astype(BF16)
    kept_ref[0] = mixed[:, width:]

    window_i = lax.rem(lax.broadcasted_iota(jnp.int32, (rows, rows), 0), cols) // WC
    window_j = lax.rem(lax.broadcasted_iota(jnp.int32, (rows, rows), 1), cols) // WC
    same = window_i == window_j
    scale = HEAD ** (-0.5)
    grads = [[], [], []]
    for h in range(heads):
        q, k, v = (
            proj_ref[0, :, (i * heads + h) * HEAD : (i * heads + h + 1) * HEAD] for i in range(3)
        )
        go = grad_out[:, h * HEAD : (h + 1) * HEAD]
        scores = lax.dot_general(q, k, NT, preferred_element_type=F32) * scale
        weights = jnp.where(same, jnp.exp(scores), 0.0)
        weights = weights / jnp.sum(weights, axis=-1, keepdims=True)
        rounded = weights.astype(BF16)
        first = (((0,), (0,)), ((), ()))
        grads[2].append(
            lax.dot_general(rounded, go, first, preferred_element_type=F32).astype(BF16)
        )
        grad_weights = lax.dot_general(go, v, NT, preferred_element_type=F32)
        inner = jnp.sum(weights * grad_weights, axis=-1, keepdims=True)
        score_round = (weights * (grad_weights - inner) * scale).astype(BF16)
        grads[0].append(jnp.dot(score_round, k, preferred_element_type=F32).astype(BF16))
        grads[1].append(
            lax.dot_general(score_round, q, first, preferred_element_type=F32).astype(BF16)
        )
    stacked = jnp.concatenate(grads[0] + grads[1] + grads[2], axis=1)
    grad_normed = lax.dot_general(stacked, w_ref[...], NT, preferred_element_type=F32)

    values = tok_ref[0].astype(F32)
    centred = values - jnp.mean(values, axis=-1, keepdims=True)
    inv_std = lax.rsqrt(jnp.mean(centred * centred, axis=-1, keepdims=True) + NORM_EPSILON)
    normed = centred * inv_std
    scaled = grad_normed * gain_ref[...]
    local = inv_std * (
        scaled
        - jnp.mean(scaled, axis=-1, keepdims=True)
        - normed * jnp.mean(scaled * normed, axis=-1, keepdims=True)
    )
    local = local.astype(BF16)
    share = local.shape[1] // (loss_count * var_count)
    for l in range(loss_count):
        for v in range(var_count):
            at = (l * var_count + v) * share
            part_ref[0, v, l] = local[:, at : at + share]


def attention_backward(f_rolled, coeff, mix, projected, tokens, gain, w_flat, groups):
    blocks, rows, model = tokens.shape
    pairs = coeff.shape[0]
    cols = rows // WR
    per_pair = blocks // pairs
    depth = f_rolled.shape[2]
    width = projected.shape[2] // 3
    heads = width // HEAD
    loss_count, var_count = groups
    share = model // (loss_count * var_count)

    def whole(shape):
        return pl.BlockSpec(shape, lambda b: (0,) * len(shape))

    def per_block(shape):
        return pl.BlockSpec((1,) + shape, lambda b: (b,) + (0,) * len(shape))

    return pl.pallas_call(
        functools.partial(attention_kernel, heads, cols, groups),
        grid=(blocks,),
        in_specs=[
            pl.BlockSpec((4, cols, depth), lambda b: (0, lax.rem(b, per_pair), 0)),
            pl.BlockSpec((1,) + coeff.shape[1:], lambda b: (b // per_pair, 0, 0)),
            whole(mix.shape),
            per_block((rows, 3 * width)),
            per_block((rows, model)),
            whole(gain.shape),
            whole(w_flat.shape),
        ],
        out_specs=(
            per_block((var_count, loss_count, rows, share)),
            per_block((rows, share)),
        ),
        out_shape=(
            jax.ShapeDtypeStruct((blocks, var_count, loss_count, rows, share), BF16),
            jax.ShapeDtypeStruct((blocks, rows, share), F32),
        ),
        name="attention_backward",
    )(f_rolled, coeff, mix, projected, tokens, gain, w_flat)


def body(tokens, shift, w_qkv, w_proj, ln_gain, w_dec, prediction, target, legendre):
    sizes = {name: lax.axis_size(name) for name in ("proc", "loss", "vars")}
    procs = sizes["proc"]
    groups = (sizes["loss"], sizes["vars"])
    group_count = groups[0] * groups[1]
    modes = legendre.shape[0]
    lat_all = legendre.shape[1]
    modes_all = modes * procs
    var_count, lats = prediction.shape[0], prediction.shape[1]
    basis = fourier_basis(modes_all)
    row_count, col_count, model = tokens.shape
    offset = shift[0]
    head_local = w_qkv.shape[2]
    width = head_local * HEAD
    share = model // group_count

    to_modes = jnp.asarray(
        basis.reshape(2, LON, procs, modes).transpose(2, 0, 3, 1).reshape(-1, LON), F32
    )
    fields = jnp.concatenate([prediction.astype(F32), target]).reshape(-1, LON)
    spectra = lax.dot_general(to_modes, fields, NT, precision=HIGHEST)
    at_owner = exchange(spectra.reshape(procs, 2 * modes, -1), "proc", sizes, 1)
    at_owner = at_owner.reshape(procs, 2, modes, 2, var_count, lats).transpose(2, 3, 1, 4, 0, 5)
    harm, power = harmonics(at_owner.reshape(modes, 4 * var_count, lat_all), legendre)
    if power.size % (procs * 128) == 0:
        shaped = power.reshape(procs, -1, 128)
        power = proc_total(shaped, sizes, 2).reshape(power.shape)
    else:
        power = lax.psum(power, "proc")
    degree_terms, pullback = jax.vjp(amse_terms, power[0], power[1], power[2])
    amse = jnp.sum(degree_terms, axis=-1) / (LDEG * modes_all)
    weight_grad = lat_all * LON / (VARS * LDEG * modes_all)
    grad_pred, _, grad_cross = pullback(jnp.full(degree_terms.shape, weight_grad, F32))
    grad_spectra, pack = spectra_grad(harm, legendre, grad_pred, grad_cross, procs)
    banded = exchange(grad_spectra, "proc", sizes, 3)
    banded = banded.reshape(procs, modes // pack, lats, pack, 2, var_count)
    banded = banded.transpose(0, 1, 3, 4, 5, 2).reshape(2 * modes_all, var_count, lats)

    pairs = row_count // WR
    sent = banded.astype(BF16).reshape(2 * modes_all, var_count, pairs, WR, 4)
    sent = sent.transpose(0, 2, 3, 1, 4).reshape(2 * modes_all, -1)
    coeff = exchange(sent, "group", sizes, 4, spread=True)
    coeff = coeff.reshape(group_count, 2 * modes_all, pairs, WR, 4 * var_count)
    coeff = coeff.transpose(2, 1, 3, 0, 4).reshape(pairs, 2 * modes_all, -1)

    by_mode = basis.transpose(1, 2, 0).reshape(LON, 2 * modes_all)
    field_grad = lax.dot_general(
        banded.reshape(2 * modes_all, -1),
        jnp.asarray(by_mode, F32),
        (((0,), (1,)), ((), ())),
        precision=HIGHEST,
    ).reshape(var_count, lats, LON)

    decoder = w_dec.transpose(2, 0, 1, 3).reshape(4 * var_count * 4, model)
    through = lax.dot_general(
        decoder, w_proj.reshape(-1, model), NT, preferred_element_type=F32
    ).astype(BF16)
    mix = jnp.concatenate(
        [
            through.reshape(-1, group_count, width),
            decoder.reshape(-1, group_count, share),
        ],
        axis=2,
    ).transpose(1, 0, 2)
    mix = exchange(mix, "group", sizes, 5)
    mix = mix.reshape(group_count, 4, 4 * var_count, width + share).transpose(1, 0, 2, 3)
    mix = mix.reshape(-1, width + share)

    cols = 120
    split = (pairs, WR, col_count // cols, cols)
    rolled = jnp.roll(tokens, -offset, axis=1)
    rolled = rolled.reshape(split + (model,)).transpose(0, 2, 1, 3, 4)
    rolled = rolled.reshape(-1, WR * cols, model)
    values = rolled.astype(F32)
    centred = values - jnp.mean(values, axis=-1, keepdims=True)
    inv_std = lax.rsqrt(jnp.mean(centred * centred, axis=-1, keepdims=True) + NORM_EPSILON)
    norm_out = (centred * inv_std * ln_gain).astype(BF16)
    w_flat = w_qkv.reshape(model, 3 * width)
    projected = jnp.einsum(
        "brd,dk->brk", norm_out, w_flat, preferred_element_type=F32
    ).astype(BF16)
    by_column = jnp.asarray(
        by_mode.reshape(col_count, 4, 2 * modes_all).transpose(1, 0, 2), BF16
    )
    f_rolled = jnp.roll(by_column, -offset, axis=1)
    parts, kept = attention_backward(
        f_rolled, coeff, mix, projected, rolled, ln_gain.reshape(1, model), w_flat, groups
    )
    summed = reduce_group(parts, kept, sizes, 6)
    summed = summed.reshape(pairs, col_count // cols, WR, cols, share).transpose(0, 2, 1, 3, 4)
    input_grad = jnp.roll(summed.reshape(row_count, col_count, share), offset, axis=1)
    return (amse, field_grad, input_grad)


def solution(mesh):
    return jax.shard_map(
        body,
        mesh=mesh,
        in_specs=(
            P("proc", None, None),
            P(),
            P(None, None, ("loss", "vars"), None),
            P(),
            P(),
            P(("loss", "vars"), None, None, None),
            P(("loss", "vars"), "proc", None),
            P(("loss", "vars"), "proc", None),
            P("proc", None, None),
        ),
        out_specs=(
            P(("loss", "vars")),
            P(("loss", "vars"), "proc", None),
            P("proc", None, ("loss", "vars")),
        ),
        check_vma=False,
    )
```

profile of v0, /device:TPU:0, one launch (start us, length us, event | category | flops | bytes accessed | tf_op | source)
XLA Modules:
  0.0 171.6 jit_solution(15812973807591266857)
XLA Ops:
  1.3 1.3 reshape.152.gain_ref
  2.6 2.2 %constant_dynamic-slice_fusion.f_ref = bf16[4,360,256]{2,1,0:T(8,128)(2,1)} fusion(bf16[4,720,256]{2,1,0:T(8,128)(2,1)} %constant.78, s32[]{:T(128)S(6)} %select_n.43), kind=kLoop, calls=%fused_computation.46 | loop fusion | bytes 1474564 | tf_op jit(solution)/shard_map/jit(_roll_dynamic)/dynamic_slice | solution.py:497
  4.8 1.4 copy.50
  6.2 0.3 reshape_reshape.7
  6.5 0.2 reshape.144
  6.7 3.7 %convolution_convert_fusion.1 = bf16[256,1536]{1,0:T(8,128)(2,1)S(1)} fusion(bf16[256,1536]{1,0:T(8,128)(2,1)S(1)} %reshape.144, bf16[1536,1536]{1,0:T(8,128)(2,1)} %bitcast.146), kind=kOutput, calls=%fused_computation.10 | convolution fusion | flops 1208352768 | bytes 6291456 | tf_op jit(solution)/shard_map/dot_general | solution.py:467
  10.4 0.3 copy.51
  10.7 0.4 copy.53
  11.1 0.1 copy.54
  11.2 1.3 maximum_bitcast_fusion.2.x_ref
  12.5 23.0 %exchange_5.1 = bf16[4,256,768]{2,1,0:T(8,128)(2,1)} custom-call(bf16[4,256,768]{2,1,0:T(8,128)(2,1)} %maximum_bitcast_fusion.2.x_ref), custom_call_target="tpu_custom_call" | custom-call | tf_op jit(solution)/shard_map/exchange_5/pallas_call | solution.py:95
  35.5 0.0 copy-start.4
  35.5 0.0 copy-start.2
  35.5 0.0 copy-start.3
  35.5 2.9 %copy.55 = bf16[4,4,64,768]{3,2,0,1:T(8,128)(2,1)} copy(bf16[4,4,64,768]{3,2,1,0:T(8,128)(2,1)} %bitcast.133) | data formatting | bytes 3145728 | tf_op jit(solution)/shard_map/reshape | solution.py:478
  38.4 0.0 copy-done.4
  38.4 0.1 convert_element_type.34
  38.5 0.0 copy-done.2
  38.5 0.0 copy-done.3
  38.5 2.2 %fusion.6 = f32[256,256]{1,0:T(8,128)} fusion(f32[256,1440]{1,0:T(8,128)S(1)} %copy-done.2, f32[16,8,1440]{2,1,0:T(8,128)S(1)} %copy-done.3, f32[16,8,1440]{2,1,0:T(8,128)S(1)} %convert_element_type.34), kind=kOutput, calls=%fused_computation.13 | convolution fusion | flops 1132830720 | bytes 3211264 | tf_op jit(solution)/shard_map/dot_general | solution.py:433
  40.7 11.8 %exchange_1.1 = f32[8,32,256]{2,1,0:T(8,128)} custom-call(f32[8,32,256]{2,1,0:T(8,128)} %bitcast.143), custom_call_target="tpu_custom_call" | custom-call | tf_op jit(solution)/shard_map/exchange_1/pallas_call | solution.py:95
  52.5 1.3 copy.40
  53.8 2.5 %reshape.136 = f32[8,2,16,2,16,8]{2,1,5,4,3,0:T(2,128)} reshape(f32[8,32,256]{1,2,0:T(8,128)S(1)} %copy.40) | data formatting | bytes 524288 | tf_op jit(solution)/shard_map/reshape | solution.py:435
  56.3 4.3 %copy.41 = f32[16,2,2,16,8,8]{3,2,1,5,4,0:T(2,128)S(1)} copy(f32[16,2,2,16,8,8]{0,2,5,3,1,4:T(2,128)} %bitcast.130) | data formatting | bytes 524288 | tf_op jit(solution)/shard_map/transpose | solution.py:435
  60.7 1.6 reshape.137
  62.3 1.0 copy.42.spectra_ref
  63.3 4.2 %harmonics.1 = (f32[16,64,384]{2,1,0:T(8,128)}, f32[3,16,384]{2,1,0:T(8,128)}) custom-call(f32[16,64,64]{2,1,0:T(8,128)} %copy.42.spectra_ref, f32[16,64,384]{2,1,0:T(8,128)} %legendre_ref.3), custom_call_target="tpu_custom_call" | custom-call | tf_op jit(solution)/shard_map/harmonics/pallas_call | solution.py:261
  67.4 1.5 reshape.138.x_ref
  68.9 15.7 %proc_total.1 = f32[8,18,128]{2,1,0:T(8,128)} custom-call(f32[8,18,128]{2,1,0:T(8,128)} %reshape.138.x_ref), custom_call_target="tpu_custom_call" | custom-call | tf_op jit(solution)/shard_map/proc_total/pallas_call | solution.py:147
  84.6 0.9 reshape.139
  85.5 0.8 bitcast_divide_fusion
  86.3 4.0 %spectra_grad.1.x_ref = f32[8,4,8,128]{3,2,1,0:T(8,128)} custom-call(f32[16,64,384]{2,1,0:T(8,128)} %get-tuple-element.8.harm_ref, f32[16,64,384]{2,1,0:T(8,128)} %legendre_ref.3, f32[16,384]{1,0:T(8,128)} %get-tuple-element.12.gp_ref, f32[16,384]{1,0:T(8,128)} %get-tuple-element.11.gc_ref), custom_call_target="tpu_custom_call" | custom-call | tf_op jit(solution)/shard_map/spectra_grad/pallas_call | solution.py:297
  90.3 8.1 %exchange_3.1 = f32[8,4,8,128]{3,2,1,0:T(8,128)} custom-call(f32[8,4,8,128]{3,2,1,0:T(8,128)} %spectra_grad.1.x_ref), custom_call_target="tpu_custom_call" | custom-call | tf_op jit(solution)/shard_map/exchange_3/pallas_call | solution.py:95
  98.5 0.5 broadcast_multiply_fusion.1
  99.0 2.2 %reshape.140 = f32[8,4,8,4,2,16]{5,4,3,2,1,0:T(2,128)S(1)} reshape(f32[8,4,8,128]{3,2,1,0:T(8,128)} %exchange_3.1) | data formatting | bytes 262144 | tf_op jit(solution)/shard_map/reshape | solution.py:448
  101.2 0.2 copy.63
  101.5 0.3 copy.46
  101.8 0.7 copy.47.x_ref
  102.6 6.6 %exchange_4.1 = bf16[4,256,128]{2,1,0:T(8,128)(2,1)} custom-call(bf16[256,128]{1,0:T(8,128)(2,1)} %copy.47.x_ref), custom_call_target="tpu_custom_call" | custom-call | tf_op jit(solution)/shard_map/exchange_4/pallas_call | solution.py:95
  109.1 1.1 copy.48
  110.3 0.8 copy.58.coeff_ref
  111.1 1.1 copy.61
  112.2 1.0 reshape_reshape.6
  113.2 0.0 copy-start.1
  113.2 0.1 copy.45
  113.3 3.9 %fusion.10 = f32[16,8,1440]{2,1,0:T(8,128)} fusion(f32[1440,256,1]{1,0,2:T(8,128)} %constant.79, f32[128,256]{1,0:T(8,128)S(1)} %copy.45), kind=kOutput, calls=%fused_computation.21 | convolution fusion | flops 566231040 | bytes 2342912 | tf_op jit(solution)/shard_map/dot_general | solution.py:459
  117.2 0.0 copy-done.1
  117.2 2.1 %fusion.5 = bf16[2,360,1536]{2,1,0:T(8,128)(2,1)S(1)} fusion(s32[]{:T(128)S(6)} %select_n.43, bf16[2,360,1536]{2,1,0:T(8,128)(2,1)S(1)} %copy-done.1), kind=kLoop, calls=%fused_computation.11 | loop fusion | flops 4423680 | bytes 4423684 | tf_op jit(solution)/shard_map/jit(_roll_dynamic)/concatenate | solution.py:483
  119.3 0.0 copy-start.5
  119.3 0.4 convert_reduce_fusion
  119.7 0.7 fusion.2
  120.4 0.0 copy-done.5
  120.4 0.7 fusion.4
  121.1 1.6 copy.57
  122.7 0.0 copy-start
  122.7 0.2 copy.56
  122.9 1.8 %copy-done = bf16[1536,3,4,96]{0,3,2,1:T(8,128)(2,1)S(1)} copy-done((bf16[1536,3,4,96]{0,3,2,1:T(8,128)(2,1)S(1)}, bf16[1536,3,4,96]{0,3,2,1:T(8,128)(2,1)}, u32[]{:S(2)}) %copy-start) | copy-done | bytes 3538968
  124.7 4.2 %convolution_convert_fusion.proj_ref = bf16[3,240,1152]{2,1,0:T(8,128)(2,1)} fusion(bf16[3,240,1536]{2,1,0:T(8,128)(2,1)S(1)} %bitcast.137, bf16[1536,1152,1]{0,1,2:T(8,128)(2,1)S(1)} %bitcast.134), kind=kOutput, calls=%fused_computation.9 | convolution fusion | flops 2548869120 | bytes 7409664 | tf_op jit(solution)/shard_map/brd,dk->brk/dot_general | solution.py:491
  128.9 3.8 %copy.59.w_ref = bf16[1536,1152]{1,0:T(8,128)(2,1)} copy(bf16[1536,1152]{0,1:T(8,128)(2,1)S(1)} %bitcast.135) | data formatting | bytes 7077888 | tf_op jit(solution)/shard_map/reshape | solution.py:490
  132.8 16.9 %attention_backward.1 = (bf16[3,2,2,240,384]{4,3,2,1,0:T(8,128)(2,1)}, f32[3,240,384]{2,1,0:T(8,128)}) custom-call(bf16[4,360,256]{2,1,0:T(8,128)(2,1)} %constant_dynamic-slice_fusion.f_ref, bf16[1,256,512]{2,1,0:T(8,128)(2,1)} %copy.58.coeff_ref, bf16[1024,768]{1,0:T(8,128)(2,1)} %bitcast.132, bf16[3,240,1152]{2,1,0:T(8,128)(2,1)} %convolution_convert_fusion.proj_ref, ...), custom_call_target="tpu_custom_call" | custom-call | tf_op jit(solution)/shard_map/attention_backward/pallas_call | solution.py:389
  149.6 19.3 %reduce_group.1 = bf16[3,240,384]{2,1,0:T(8,128)(2,1)} custom-call(bf16[3,2,2,240,384]{4,3,2,1,0:T(8,128)(2,1)} %get-tuple-element.9.p_ref, f32[3,240,384]{2,1,0:T(8,128)} %get-tuple-element.10.kept_ref), custom_call_target="tpu_custom_call" | custom-call | tf_op jit(solution)/shard_map/reduce_group/pallas_call | solution.py:223
  169.0 1.1 copy.60
  170.1 1.5 fusion.9
  (4 shorter events, 0.1 us)
Async XLA Ops:
  35.5 2.9 %copy-start.4 = (bf16[16,8,1440]{2,1,0:T(8,128)(2,1)S(1)}, bf16[16,8,1440]{2,1,0:T(8,128)(2,1)}, u32[]{:S(2)}) copy-start(bf16[16,8,1440]{2,1,0:T(8,128)(2,1)} %param.18) | copy-start | bytes 1105924
  35.5 3.0 %copy-start.2 = (f32[256,1440]{1,0:T(8,128)S(1)}, f32[256,1440]{1,0:T(8,128)}, u32[]{:S(2)}) copy-start(f32[256,1440]{1,0:T(8,128)} %constant.74.clone) | copy-start | bytes 4423684
  35.5 3.0 %copy-start.3 = (f32[16,8,1440]{2,1,0:T(8,128)S(1)}, f32[16,8,1440]{2,1,0:T(8,128)}, u32[]{:S(2)}) copy-start(f32[16,8,1440]{2,1,0:T(8,128)} %param.19) | copy-start | bytes 2211844
  113.2 4.0 %copy-start.1 = (bf16[2,360,1536]{2,1,0:T(8,128)(2,1)S(1)}, bf16[2,360,1536]{2,1,0:T(8,128)(2,1)}, u32[]{:S(2)}) copy-start(bf16[2,360,1536]{2,1,0:T(8,128)(2,1)} %param.12) | copy-start | bytes 6635524
  119.3 1.1 copy-start.5
  122.7 2.0 %copy-start = (bf16[1536,3,4,96]{0,3,2,1:T(8,128)(2,1)S(1)}, bf16[1536,3,4,96]{0,3,2,1:T(8,128)(2,1)}, u32[]{:S(2)}) copy-start(bf16[1536,3,4,96]{0,3,2,1:T(8,128)(2,1)} %param.14) | copy-start | bytes 10616836
where the time goes:
time: 172 us
  Pallas kernels  110 us (64%)
  local copies, waits for them, and re-layouts  38.4 us (22%)
  matrix products  14 us (8%)
  other arithmetic  8.1 us (5%)
    pallas_call x4, Pallas kernels, exchange(): pl.pallas_call(functools.partial(exchange_kernel, axis, count, sizes, spr...  49.5 us
    pallas_call x1, Pallas kernels, reduce_group(): pl.pallas_call(functools.partial(scatter_kernel, blocks, sizes), out_shap...  19.3 us
    pallas_call x1, Pallas kernels, attention_backward(): pl.pallas_call(functools.partial(attention_kernel, heads, cols, groups),...  16.9 us
    pallas_call x1, Pallas kernels, proc_total(): pl.pallas_call(functools.partial(total_kernel, count, sizes), out_shape=j...  15.7 us
    transpose x1, local copies, waits for them, and re-layouts, body(): at_owner.reshape(procs, 2, modes, 2, var_count, lats)  4.35 us
    dot_general x1, matrix products, body(): jnp.einsum('brd,dk->brk', norm_out, w_flat, preferred_element_type=F32)  4.17 us
    pallas_call x1, Pallas kernels, harmonics(): pl.pallas_call(functools.partial(harmonics_kernel, modes, var_count), out...  4.15 us
    pallas_call x1, Pallas kernels, spectra_grad(): pl.pallas_call(functools.partial(spectra_grad_kernel, modes, pack, procs,...  4 us

commit v1 on v0

--- a/solution.py
+++ b/solution.py
@@ -74,7 +74,7 @@
         copies.append(
             pltpu.make_async_remote_copy(
                 src_ref=x_ref if spread else x_ref.at[peer],
-                dst_ref=out_ref.at[me],
+                dst_ref=out_ref.at[k + 1] if spread else out_ref.at[me],
                 send_sem=send.at[k],
                 recv_sem=recv.at[k],
                 device_id=place(axis, peer, sizes),
@@ -82,7 +82,10 @@
             )
         )
         copies[-1].start()
-    local = pltpu.make_async_copy(x_ref if spread else x_ref.at[me], out_ref.at[me], own)
+    if spread:
+        local = pltpu.make_async_copy(x_ref, out_ref.at[0], own)
+    else:
+        local = pltpu.make_async_copy(x_ref.at[me], out_ref.at[me], own)
     local.start()
     local.wait()
     for copy in copies:
@@ -160,85 +163,6 @@
         ),
         name="proc_total",
     )(x)
-
-
-def scatter_kernel(blocks, sizes, p_ref, kept_ref, out_ref, got, mid, far, s1, r1, s2, r2):
-    loss_count, var_count = sizes["loss"], sizes["vars"]
-    loss, var = lax.axis_index("loss"), lax.axis_index("vars")
-    near = [lax.rem(var + k, var_count) for k in range(1, var_count)]
-    away = [lax.rem(loss + k, loss_count) for k in range(1, loss_count)]
-    greet(
-        [place("vars", peer, sizes) for peer in near]
-        + [place("loss", peer, sizes) for peer in away]
-    )
-    first, second = [], []
-    for b in range(blocks):
-        row = []
-        for k, peer in enumerate(near):
-            row.append(
-                pltpu.make_async_remote_copy(
-                    src_ref=p_ref.at[b, peer],
-                    dst_ref=got.at[b, k],
-                    send_sem=s1.at[b, k],
-                    recv_sem=r1.at[b, k],
-                    device_id=place("vars", peer, sizes),
-                    device_id_type=MESH,
-                )
-            )
-            row[-1].start()
-        first.append(row)
-    for b in range(blocks):
-        for made in first[b]:
-            made.wait()
-        for j in range(loss_count):
-            value = p_ref[b, var, j].astype(F32)
-            for k in range(var_count - 1):
-                value = value + got[b, k, j].astype(F32)
-            mid[b, j] = value.astype(BF16)
-        row = []
-        for k, peer in enumerate(away):
-            row.append(
-                pltpu.make_async_remote_copy(
-                    src_ref=mid.at[b, peer],
-                    dst_ref=far.at[b, k],
-                    send_sem=s2.at[b, k],
-                    recv_sem=r2.at[b, k],
-                    device_id=place("loss", peer, sizes),
-                    device_id_type=MESH,
-                )
-            )
-            row[-1].start()
-        second.append(row)
-    for b in range(blocks):
-        value = kept_ref[b] + mid[b, loss].astype(F32)
-        for made in second[b]:
-            made.wait()
-        for k in range(loss_count - 1):
-            value = value + far[b, k].astype(F32)
-        out_ref[b] = value.astype(BF16)
-
-
-def reduce_group(parts, kept, sizes, collective_id):
-    blocks, var_count, loss_count, rows, width = parts.shape
-    return pl.pallas_call(
-        functools.partial(scatter_kernel, blocks, sizes),
-        out_shape=jax.ShapeDtypeStruct(kept.shape, BF16),
-        in_specs=[VMEM, VMEM],
-        out_specs=VMEM,
-        scratch_shapes=[
-            pltpu.VMEM((blocks, var_count - 1, loss_count, rows, width), BF16),
-            pltpu.VMEM((blocks, loss_count, rows, width), BF16),
-            pltpu.VMEM((blocks, loss_count - 1, rows, width), BF16),
-            pltpu.SemaphoreType.DMA((blocks, var_count - 1)),
-            pltpu.SemaphoreType.DMA((blocks, var_count - 1)),
-            pltpu.SemaphoreType.DMA((blocks, loss_count - 1)),
-            pltpu.SemaphoreType.DMA((blocks, loss_count - 1)),
-        ],
-        compiler_params=pltpu.CompilerParams(
-            collective_id=collective_id, has_side_effects=True
-        ),
-        name="reduce_group",
-    )(parts, kept)
 
 
 def harmonics_kernel(modes, var_count, spectra_ref, legendre_ref, harm_ref, power_ref):
@@ -306,10 +230,79 @@
 
 
 def attention_kernel(
-    heads, cols, groups, f_ref, coeff_ref, mix_ref, proj_ref, tok_ref, gain_ref, w_ref, part_ref, kept_ref
+    heads,
+    cols,
+    blocks,
+    sizes,
+    f_ref,
+    coeff_ref,
+    mix_ref,
+    proj_ref,
+    tok_ref,
+    gain_ref,
+    w_ref,
+    out_ref,
+    part,
+    kept,
+    got,
+    mid,
+    far,
+    s1,
+    r1,
+    s2,
+    r2,
 ):
-    loss_count, var_count = groups
+    loss_count, var_count = sizes["loss"], sizes["vars"]
+    loss, var = lax.axis_index("loss"), lax.axis_index("vars")
+    near = [lax.rem(var + k, var_count) for k in range(1, var_count)]
+    away = [lax.rem(loss + k, loss_count) for k in range(1, loss_count)]
+    step = pl.program_id(0)
     rows = WR * cols
+
+    @pl.when(step == 0)
+    def _():
+        greet(
+            [place("vars", peer, sizes) for peer in near]
+            + [place("loss", peer, sizes) for peer in away]
+        )
+
+    def near_copies(b):
+        return [
+            pltpu.make_async_remote_copy(
+                src_ref=part.at[b, peer],
+                dst_ref=got.at[b, k],
+                send_sem=s1.at[b, k],
+                recv_sem=r1.at[b, k],
+                device_id=place("vars", peer, sizes),
+                device_id_type=MESH,
+            )
+            for k, peer in enumerate(near)
+        ]
+
+    def away_copies(b):
+        return [
+            pltpu.make_async_remote_copy(
+                src_ref=mid.at[b, peer],
+                dst_ref=far.at[b, k],
+                send_sem=s2.at[b, k],
+                recv_sem=r2.at[b, k],
+                device_id=place("loss", peer, sizes),
+                device_id_type=MESH,
+            )
+            for k, peer in enumerate(away)
+        ]
+
+    def pass_on(b):
+        for made in near_copies(b):
+            made.wait()
+        for j in range(loss_count):
+            value = part[b, var, j].astype(F32)
+            for k in range(var_count - 1):
+                value = value + got[b, k, j].astype(F32)
+            mid[b, j] = value.astype(BF16)
+        for made in away_copies(b):
+            made.start()
+
     pieces = []
     for o in range(4):
         y = jnp.dot(f_ref[o], coeff_ref[0], preferred_element_type=F32)
@@ -321,7 +314,7 @@
     mixed = jnp.dot(tiles, mix_ref[...], preferred_element_type=F32)
     width = heads * HEAD
     grad_out = mixed[:, :width].astype(BF16)
-    kept_ref[0] = mixed[:, width:]
+    kept[step] = mixed[:, width:]
 
     window_i = lax.rem(lax.broadcasted_iota(jnp.int32, (rows, rows), 0), cols) // WC
     window_j = lax.rem(lax.broadcasted_iota(jnp.int32, (rows, rows), 1), cols) // WC
@@ -366,10 +359,27 @@
     for l in range(loss_count):
         for v in range(var_count):
             at = (l * var_count + v) * share
-            part_ref[0, v, l] = local[:, at : at + share]
-
-
-def attention_backward(f_rolled, coeff, mix, projected, tokens, gain, w_flat, groups):
+            part[step, v, l] = local[:, at : at + share]
+    for made in near_copies(step):
+        made.start()
+
+    @pl.when(step > 0)
+    def _():
+        pass_on(step - 1)
+
+    @pl.when(step == blocks - 1)
+    def _():
+        pass_on(blocks - 1)
+        for b in range(blocks):
+            for made in away_copies(b):
+                made.wait()
+            value = kept[b] + mid[b, loss].astype(F32)
+            for k in range(loss_count - 1):
+                value = value + far[b, k].astype(F32)
+            out_ref[b] = value.astype(BF16)
+
+
+def attention_backward(f_rolled, coeff, mix, projected, tokens, gain, w_flat, sizes, collective_id):
     blocks, rows, model = tokens.shape
     pairs = coeff.shape[0]
     cols = rows // WR
@@ -377,7 +387,7 @@
     depth = f_rolled.shape[2]
     width = projected.shape[2] // 3
     heads = width // HEAD
-    loss_count, var_count = groups
+    loss_count, var_count = sizes["loss"], sizes["vars"]
     share = model // (loss_count * var_count)
 
     def whole(shape):
@@ -387,7 +397,7 @@
         return pl.BlockSpec((1,) + shape, lambda b: (b,) + (0,) * len(shape))
 
     return pl.pallas_call(
-        functools.partial(attention_kernel, heads, cols, groups),
+        functools.partial(attention_kernel, heads, cols, blocks, sizes),
         grid=(blocks,),
         in_specs=[
             pl.BlockSpec((4, cols, depth), lambda b: (0, lax.rem(b, per_pair), 0)),
@@ -398,13 +408,21 @@
             whole(gain.shape),
             whole(w_flat.shape),
         ],
-        out_specs=(
-            per_block((var_count, loss_count, rows, share)),
-            per_block((rows, share)),
-        ),
-        out_shape=(
-            jax.ShapeDtypeStruct((blocks, var_count, loss_count, rows, share), BF16),
-            jax.ShapeDtypeStruct((blocks, rows, share), F32),
+        out_specs=whole((blocks, rows, share)),
+        out_shape=jax.ShapeDtypeStruct((blocks, rows, share), BF16),
+        scratch_shapes=[
+            pltpu.VMEM((blocks, var_count, loss_count, rows, share), BF16),
+            pltpu.VMEM((blocks, rows, share), F32),
+            pltpu.VMEM((blocks, var_count - 1, loss_count, rows, share), BF16),
+            pltpu.VMEM((blocks, loss_count, rows, share), BF16),
+            pltpu.VMEM((blocks, loss_count - 1, rows, share), BF16),
+            pltpu.SemaphoreType.DMA((blocks, var_count - 1)),
+            pltpu.SemaphoreType.DMA((blocks, var_count - 1)),
+            pltpu.SemaphoreType.DMA((blocks, loss_count - 1)),
+            pltpu.SemaphoreType.DMA((blocks, loss_count - 1)),
+        ],
+        compiler_params=pltpu.CompilerParams(
+            collective_id=collective_id, has_side_effects=True
         ),
         name="attention_backward",
     )(f_rolled, coeff, mix, projected, tokens, gain, w_flat)
@@ -474,11 +492,17 @@
         ],
         axis=2,
     ).transpose(1, 0, 2)
-    mix = exchange(mix, "group", sizes, 5)
+    me = rank("group", sizes)
+    received = [lax.dynamic_index_in_dim(mix, me, 0, keepdims=False)]
+    for k in range(1, group_count):
+        block = lax.dynamic_index_in_dim(mix, lax.rem(me + k, group_count), 0, keepdims=False)
+        ring = [(g, (g + k) % group_count) for g in range(group_count)]
+        received.append(lax.ppermute(block, ("loss", "vars"), ring))
+    mix = jnp.stack(received)
     mix = mix.reshape(group_count, 4, 4 * var_count, width + share).transpose(1, 0, 2, 3)
     mix = mix.reshape(-1, width + share)
 
-    cols = 120
+    cols = 72
     split = (pairs, WR, col_count // cols, cols)
     rolled = jnp.roll(tokens, -offset, axis=1)
     rolled = rolled.reshape(split + (model,)).transpose(0, 2, 1, 3, 4)
@@ -495,10 +519,9 @@
         by_mode.reshape(col_count, 4, 2 * modes_all).transpose(1, 0, 2), BF16
     )
     f_rolled = jnp.roll(by_column, -offset, axis=1)
-    parts, kept = attention_backward(
-        f_rolled, coeff, mix, projected, rolled, ln_gain.reshape(1, model), w_flat, groups
+    summed = attention_backward(
+        f_rolled, coeff, mix, projected, rolled, ln_gain.reshape(1, model), w_flat, sizes, 6
     )
-    summed = reduce_group(parts, kept, sizes, 6)
     summed = summed.reshape(pairs, col_count // cols, WR, cols, share).transpose(0, 2, 1, 3, 4)
     input_grad = jnp.roll(summed.reshape(row_count, col_count, share), offset, axis=1)
     return (amse, field_grad, input_grad)

time: 172 us -> 158 us (0.919)
  Pallas kernels: 110 us -> 80.3 us
  local copies, waits for them, and re-layouts: 38.4 us -> 46.9 us
  starting transfers between devices: 0 us -> 4.43 us
    pallas_call x4 -> x3, Pallas kernels: 49.5 us -> 25.3 us  [exchange(): pl.pallas_call(functools.partial(exchange_kernel, axis, count, sizes, spr...]
    pallas_call x2 -> x1, Pallas kernels: 36.2 us -> 31.4 us  [attention_backward(): pl.pallas_call(functools.partial(attention_kernel, heads, cols, blocks, s...]
    ppermute x0 -> x3, starting transfers between devices: none -> 4.43 us  [body(): received.append(lax.ppermute(block, ('loss', 'vars'), ring))]
    another operation x0 -> x1, local copies, waits for them, and re-layouts: none -> 3.3 us
    unnamed x12 -> x23, local copies, waits for them, and re-layouts: 1.85 us -> 4.8 us
    reshape x1 -> x0, local copies, waits for them, and re-layouts: 2.88 us -> none  [body(): mix.reshape(group_count, 4, 4 * var_count, width + share)]
    dot_general x1, matrix products: 4.17 us -> 6.03 us  [body(): jnp.einsum('brd,dk->brk', norm_out, w_flat, preferred_element_type=F32)]
  transfers between devices with their start and end apart: 0 -> 3, of which waited for: 0 -> 0; matrix products, arithmetic and copies ran while one was open for 0% -> 34% of each run, Pallas kernels for 0% -> 31%
where the time goes in v1:
time: 158 us; the launch traced here: 157 us
  Pallas kernels  80.3 us (51%)
  local copies, waits for them, and re-layouts  46.9 us (30%)
  matrix products  14.3 us (9%)
  other arithmetic  9.58 us (6%)
  starting transfers between devices  4.43 us (3%)
  between operations  1.64 us (1%)
    pallas_call x1, Pallas kernels, attention_backward(): pl.pallas_call(functools.partial(attention_kernel, heads, cols, blocks, s...  31.4 us
    pallas_call x3, Pallas kernels, exchange(): pl.pallas_call(functools.partial(exchange_kernel, axis, count, sizes, spr...  25.3 us
    pallas_call x1, Pallas kernels, proc_total(): pl.pallas_call(functools.partial(total_kernel, count, sizes), out_shape=j...  15.4 us
    dot_general x1, matrix products, body(): jnp.einsum('brd,dk->brk', norm_out, w_flat, preferred_element_type=F32)  6.03 us
    unnamed x23, local copies, waits for them, and re-layouts  4.8 us
    ppermute x3, starting transfers between devices, body(): received.append(lax.ppermute(block, ('loss', 'vars'), ring))  4.43 us
    transpose x1, local copies, waits for them, and re-layouts, body(): at_owner.reshape(procs, 2, modes, 2, var_count, lats)  4.35 us
    pallas_call x1, Pallas kernels, harmonics(): pl.pallas_call(functools.partial(harmonics_kernel, modes, var_count), out...  4.13 us
  transfers between devices with their start and end apart: 3, of which 0 were waited for; matrix products, arithmetic and copies ran while one was open for 34% of the time, Pallas kernels for 31%

profile of v1, /device:TPU:0, one launch (start us, length us, event | category | flops | bytes accessed | tf_op | source)
XLA Modules:
  0.0 157.2 jit_solution(2627263786927703943)
XLA Ops:
  0.6 1.4 copy.46
  2.1 0.3 reshape_reshape.7
  2.4 0.2 reshape.157
  2.6 3.8 %convolution_convert_fusion.1 = bf16[256,1536]{1,0:T(8,128)(2,1)S(1)} fusion(bf16[256,1536]{1,0:T(8,128)(2,1)S(1)} %reshape.157, bf16[1536,1536]{1,0:T(8,128)(2,1)} %bitcast.154), kind=kOutput, calls=%fused_computation.10 | convolution fusion | flops 1208352768 | bytes 6291456 | tf_op jit(solution)/shard_map/dot_general | solution.py:485
  6.3 0.2 reshape.159
  6.5 0.3 constant_dynamic-update-slice_fusion.1
  6.8 0.4 constant_dynamic-update-slice_fusion
  7.2 3.3 %constant_dynamic-slice_fusion.3 = (bf16[256,1,768]{2,1,0:T(2,128)(2,1)S(1)}, bf16[256,1,768]{2,1,0:T(2,128)(2,1)S(1)}, bf16[256,1,768]{2,1,0:T(2,128)(2,1)S(1)}, bf16[256,1,768]{2,1,0:T(2,128)(2,1)S(1)}) fusion(bf16[256,4,768]{2,1,0:T(4,128)(2,1)S(1)} %constant_dynamic-update-slice_fusion, s32[]{:T(128)S(6)} %select_n.57, s32[]{:T(128)S(6)} %select_n.60, ...), kind=kLoop, calls=%fused_computation.54 | loop fusion | bytes 3145744 | tf_op jit(solution)/shard_map/dynamic-slice
  10.5 0.0 copy-start.6
  10.5 0.0 copy-start.2
  10.5 0.0 copy-start.4
  10.5 0.8 copy.66
  11.3 0.5 collective-permute-start
  11.8 0.8 copy.65
  12.6 2.5 %collective-permute-start.1 = (bf16[256,768]{1,0:T(8,128)(2,1)}, bf16[256,768]{1,0:T(8,128)(2,1)}, u32[]{:S(2)}, u32[]{:S(2)}) collective-permute-start(bf16[256,768]{1,0:T(8,128)(2,1)} %bitcast.132), channel_id=1, source_target_pairs={{0,2},{1,3},{2,0},{3,1},{4,6},{5,7},{6,4},{7,5},{8,10},{9,11},{10,... | collective-permute-start | bytes 1179656 | tf_op jit(solution)/shard_map/ppermute | solution.py:500
  15.1 0.8 copy.64
  15.9 1.5 collective-permute-start.2
  18.1 0.1 convert_element_type.34
  18.2 2.2 %fusion.6 = f32[256,256]{1,0:T(8,128)} fusion(f32[256,1440]{1,0:T(8,128)S(1)} %copy-done.2, f32[16,8,1440]{2,1,0:T(8,128)S(1)} %copy-done.4, f32[16,8,1440]{2,1,0:T(8,128)S(1)} %convert_element_type.34), kind=kOutput, calls=%fused_computation.13 | convolution fusion | flops 1132830720 | bytes 3211264 | tf_op jit(solution)/shard_map/dot_general | solution.py:451
  20.4 10.6 %exchange_1.1 = f32[8,32,256]{2,1,0:T(8,128)} custom-call(f32[8,32,256]{2,1,0:T(8,128)} %bitcast.151), custom_call_target="tpu_custom_call" | custom-call | tf_op jit(solution)/shard_map/exchange_1/pallas_call | solution.py:98
  31.0 1.3 copy.36
  32.2 2.5 %reshape.149 = f32[8,2,16,2,16,8]{2,1,5,4,3,0:T(2,128)} reshape(f32[8,32,256]{1,2,0:T(8,128)S(1)} %copy.36) | data formatting | bytes 524288 | tf_op jit(solution)/shard_map/reshape | solution.py:453
  34.7 4.3 %copy.37 = f32[16,2,2,16,8,8]{3,2,1,5,4,0:T(2,128)S(1)} copy(f32[16,2,2,16,8,8]{0,2,5,3,1,4:T(2,128)} %bitcast.140) | data formatting | bytes 524288 | tf_op jit(solution)/shard_map/transpose | solution.py:453
  39.1 1.6 %reshape.150 = f32[16,64,64]{1,2,0:T(8,128)S(1)} reshape(f32[16,2,2,16,8,8]{3,2,1,5,4,0:T(2,128)S(1)} %copy.37) | data formatting | bytes 524288 | tf_op jit(solution)/shard_map/reshape | solution.py:454
  40.7 1.0 copy.38.spectra_ref
  41.7 4.1 %harmonics.1 = (f32[16,64,384]{2,1,0:T(8,128)}, f32[3,16,384]{2,1,0:T(8,128)}) custom-call(f32[16,64,64]{2,1,0:T(8,128)} %copy.38.spectra_ref, f32[16,64,384]{2,1,0:T(8,128)} %legendre_ref.3), custom_call_target="tpu_custom_call" | custom-call | tf_op jit(solution)/shard_map/harmonics/pallas_call | solution.py:185
  45.8 1.5 reshape.151.x_ref
  47.3 15.4 %proc_total.1 = f32[8,18,128]{2,1,0:T(8,128)} custom-call(f32[8,18,128]{2,1,0:T(8,128)} %reshape.151.x_ref), custom_call_target="tpu_custom_call" | custom-call | tf_op jit(solution)/shard_map/proc_total/pallas_call | solution.py:150
  62.8 0.9 reshape.152
  63.7 0.8 bitcast_divide_fusion
  64.5 4.0 %spectra_grad.1.x_ref = f32[8,4,8,128]{3,2,1,0:T(8,128)} custom-call(f32[16,64,384]{2,1,0:T(8,128)} %get-tuple-element.6.harm_ref, f32[16,64,384]{2,1,0:T(8,128)} %legendre_ref.3, f32[16,384]{1,0:T(8,128)} %get-tuple-element.12.gp_ref, f32[16,384]{1,0:T(8,128)} %get-tuple-element.11.gc_ref), custom_call_target="tpu_custom_call" | custom-call | tf_op jit(solution)/shard_map/spectra_grad/pallas_call | solution.py:221
  68.5 8.1 %exchange_3.1 = f32[8,4,8,128]{3,2,1,0:T(8,128)} custom-call(f32[8,4,8,128]{3,2,1,0:T(8,128)} %spectra_grad.1.x_ref), custom_call_target="tpu_custom_call" | custom-call | tf_op jit(solution)/shard_map/exchange_3/pallas_call | solution.py:98
  76.6 2.2 %reshape.153 = f32[8,4,8,4,2,16]{5,4,3,2,1,0:T(2,128)S(1)} reshape(f32[8,4,8,128]{3,2,1,0:T(8,128)} %exchange_3.1) | data formatting | bytes 262144 | tf_op jit(solution)/shard_map/reshape | solution.py:466
  78.9 0.2 copy.63
  79.1 1.8 %copy.54 = f32[8,4,8,4,2,16]{2,5,4,3,1,0:T(8,128)} copy(f32[8,4,8,4,2,16]{5,4,3,2,1,0:T(2,128)S(1)} %reshape.153) | data formatting | bytes 262144 | tf_op jit(solution)/shard_map/transpose | solution.py:467
  80.9 3.4 %fusion.5 = bf16[2,360,1536]{2,1,0:T(8,128)(2,1)S(1)} fusion(s32[]{:T(128)S(6)} %select_n.56, bf16[2,360,1536]{2,1,0:T(8,128)(2,1)} %param.12), kind=kLoop, calls=%fused_computation.11 | loop fusion | flops 4423680 | bytes 4423684 | tf_op jit(solution)/shard_map/jit(_roll_dynamic)/concatenate | solution.py:507
  84.4 0.4 convert_reduce_fusion
  84.8 0.0 copy-start.8
  84.8 1.6 copy.50
  86.3 0.6 reshape.164.gain_ref
  86.9 0.5 broadcast_multiply_fusion.1
  87.4 1.0 copy.42
  88.4 0.9 reshape.154
  89.3 0.7 copy.43.x_ref
  90.0 6.6 %exchange_4.1 = bf16[4,256,128]{2,1,0:T(8,128)(2,1)} custom-call(bf16[256,128]{1,0:T(8,128)(2,1)} %copy.43.x_ref), custom_call_target="tpu_custom_call" | custom-call | tf_op jit(solution)/shard_map/exchange_4/pallas_call | solution.py:98
  96.6 1.1 copy.44
  97.7 0.9 copy.51.coeff_ref
  98.6 2.6 %reshape_reshape.6 = f32[256,128]{1,0:T(8,128)S(1)} reshape(f32[8,4,4,2,16,8]{5,4,3,2,1,0:T(8,128)} %bitcast.139) | data formatting | bytes 262144 | tf_op jit(solution)/shard_map/reshape;reshape | solution.py:478
  101.2 0.8 copy.41
  102.0 0.8 copy.55
  102.8 0.7 fusion.2
  103.6 0.7 fusion.4
  104.3 0.0 copy-start
  104.3 1.5 copy.49
  105.8 1.3 copy-done
  107.1 3.8 %copy.52.w_ref = bf16[1536,1152]{1,0:T(8,128)(2,1)} copy(bf16[1536,1152]{0,1:T(8,128)(2,1)S(1)} %bitcast.142) | data formatting | bytes 7077888 | tf_op jit(solution)/shard_map/reshape | solution.py:514
  110.9 6.0 %convolution_convert_fusion.proj_ref = bf16[5,144,1152]{2,1,0:T(8,128)(2,1)} fusion(bf16[5,144,1536]{2,1,0:T(8,128)(2,1)} %bitcast.144, bf16[1536,1152,1]{0,1,2:T(8,128)(2,1)S(1)} %bitcast.143), kind=kOutput, calls=%fused_computation.9 | convolution fusion | flops 2548869120 | bytes 7409664 | tf_op jit(solution)/shard_map/brd,dk->brk/dot_general | solution.py:515
  116.9 1.1 constant_dynamic-slice_fusion.4.f_ref
  118.0 2.4 %fusion.10 = f32[16,8,1440]{2,1,0:T(8,128)} fusion(f32[1440,256,1]{1,0,2:T(8,128)S(1)} %copy-done.3, f32[128,256]{1,0:T(8,128)S(1)} %copy-done.5), kind=kOutput, calls=%fused_computation.24 | convolution fusion | flops 566231040 | bytes 2342912 | tf_op jit(solution)/shard_map/dot_general | solution.py:477
  120.4 1.4 maximum_bitcast_fusion.2
  121.8 1.3 copy.48
  123.1 31.4 %attention_backward.1 = bf16[5,144,384]{2,1,0:T(8,128)(2,1)} custom-call(bf16[4,360,256]{2,1,0:T(8,128)(2,1)} %constant_dynamic-slice_fusion.4.f_ref, bf16[1,256,512]{2,1,0:T(8,128)(2,1)} %copy.51.coeff_ref, bf16[1024,768]{1,0:T(8,128)(2,1)} %bitcast.141, bf16[5,144,1152]{2,1,0:T(8,128)(2,1)} %convolution_convert_fusion.proj_ref, ...), custom_call_target="tpu_custom_call" | custom-call | tf_op jit(solution)/shard_map/attention_backward/pallas_call | solution.py:399
  154.5 1.1 copy.53
  155.6 1.5 fusion.9
  (18 shorter events, 0.1 us)
Async XLA Ops:
  10.5 7.6 %copy-start.6 = (bf16[16,8,1440]{2,1,0:T(8,128)(2,1)S(1)}, bf16[16,8,1440]{2,1,0:T(8,128)(2,1)}, u32[]{:S(2)}) copy-start(bf16[16,8,1440]{2,1,0:T(8,128)(2,1)} %param.18) | copy-start | bytes 1105924
  10.5 7.7 %copy-start.2 = (f32[256,1440]{1,0:T(8,128)S(1)}, f32[256,1440]{1,0:T(8,128)}, u32[]{:S(2)}) copy-start(f32[256,1440]{1,0:T(8,128)} %constant.104.clone) | copy-start | bytes 4423684
  10.5 7.7 %copy-start.4 = (f32[16,8,1440]{2,1,0:T(8,128)S(1)}, f32[16,8,1440]{2,1,0:T(8,128)}, u32[]{:S(2)}) copy-start(f32[16,8,1440]{2,1,0:T(8,128)} %param.19) | copy-start | bytes 2211844
  11.3 109.0 %collective-permute-start = (bf16[256,768]{1,0:T(8,128)(2,1)}, bf16[256,768]{1,0:T(8,128)(2,1)}, u32[]{:S(2)}, u32[]{:S(2)}) collective-permute-start(bf16[256,768]{1,0:T(8,128)(2,1)} %bitcast.133), channel_id=1, source_target_pairs={{0,1},{1,2},{2,3},{3,0},{4,5},{5,6},{6,7},{7,4},{8,9},{9,10},{10,1... | collective-permute-start | bytes 1179656 | tf_op jit(solution)/shard_map/ppermute | solution.py:500
  12.6 107.7 %collective-permute-start.1 = (bf16[256,768]{1,0:T(8,128)(2,1)}, bf16[256,768]{1,0:T(8,128)(2,1)}, u32[]{:S(2)}, u32[]{:S(2)}) collective-permute-start(bf16[256,768]{1,0:T(8,128)(2,1)} %bitcast.132), channel_id=1, source_target_pairs={{0,2},{1,3},{2,0},{3,1},{4,6},{5,7},{6,4},{7,5},{8,10},{9,11},{10,... | collective-permute-start | bytes 1179656 | tf_op jit(solution)/shard_map/ppermute | solution.py:500
  15.9 104.4 %collective-permute-start.2 = (bf16[256,768]{1,0:T(8,128)(2,1)}, bf16[256,768]{1,0:T(8,128)(2,1)}, u32[]{:S(2)}, u32[]{:S(2)}) collective-permute-start(bf16[256,768]{1,0:T(8,128)(2,1)} %bitcast.131), channel_id=1, source_target_pairs={{0,3},{1,0},{2,1},{3,2},{4,7},{5,4},{6,5},{7,6},{8,11},{9,8},{10,9... | collective-permute-start | bytes 1179656 | tf_op jit(solution)/shard_map/ppermute | solution.py:500
  84.8 1.6 copy-start.8
  104.3 2.8 %copy-start = (bf16[1536,3,4,96]{0,3,2,1:T(8,128)(2,1)S(1)}, bf16[1536,3,4,96]{0,3,2,1:T(8,128)(2,1)}, u32[]{:S(2)}) copy-start(bf16[1536,3,4,96]{0,3,2,1:T(8,128)(2,1)} %param.14) | copy-start | bytes 10616836
  110.9 6.0 %copy-start.7 = (bf16[4,720,256]{2,1,0:T(8,128)(2,1)S(1)}, bf16[4,720,256]{2,1,0:T(8,128)(2,1)}, u32[]{:S(2)}) copy-start(bf16[4,720,256]{2,1,0:T(8,128)(2,1)} %constant.108) | copy-start | bytes 4423684
  110.9 7.1 %copy-start.3 = (f32[1440,256,1]{1,0,2:T(8,128)S(1)}, f32[1440,256,1]{1,0,2:T(8,128)}, u32[]{:S(2)}) copy-start(f32[1440,256,1]{1,0,2:T(8,128)} %constant.109) | copy-start | bytes 4423684
  110.9 7.1 %copy-start.5 = (f32[128,256]{1,0:T(8,128)S(1)}, f32[128,256]{1,0:T(8,128)}, u32[]{:S(2)}) copy-start(f32[128,256]{1,0:T(8,128)} %copy.41) | copy-start | bytes 393220
  116.9 3.4 %copy-start.1 = (bf16[256,1,768]{2,0,1:T(8,128)(2,1)S(1)}, bf16[256,1,768]{2,0,1:T(8,128)(2,1)}, u32[]{:S(2)}) copy-start(bf16[256,1,768]{2,0,1:T(8,128)(2,1)} %copy.55) | copy-start | bytes 1179652

commit v2 on v1

--- a/solution.py
+++ b/solution.py
@@ -109,59 +109,6 @@
             collective_id=collective_id, has_side_effects=True
         ),
         name="exchange_%d" % collective_id,
-    )(x)
-
-
-def total_kernel(count, sizes, x_ref, out_ref, parts, acc, send, recv, send2, recv2, own):
-    me = rank("proc", sizes)
-    peers = [lax.rem(me + k, count) for k in range(1, count)]
-    greet([place("proc", peer, sizes) for peer in peers])
-
-    def copy(src, dst, sems, k, peer):
-        made = pltpu.make_async_remote_copy(
-            src_ref=src,
-            dst_ref=dst,
-            send_sem=sems[0].at[k],
-            recv_sem=sems[1].at[k],
-            device_id=place("proc", peer, sizes),
-            device_id_type=MESH,
-        )
-        made.start()
-        return made
-
-    first = [copy(x_ref.at[peer], parts.at[k], (send, recv), k, peer) for k, peer in enumerate(peers)]
-    for made in first:
-        made.wait()
-    value = x_ref[me]
-    for k in range(count - 1):
-        value = value + parts[k]
-    acc[...] = value
-    second = [copy(acc, out_ref.at[me], (send2, recv2), k, peer) for k, peer in enumerate(peers)]
-    local = pltpu.make_async_copy(acc, out_ref.at[me], own)
-    local.start()
-    local.wait()
-    for made in second:
-        made.wait()
-
-
-def proc_total(x, sizes, collective_id):
-    count = sizes["proc"]
-    sems = [pltpu.SemaphoreType.DMA((count - 1,)) for _ in range(4)]
-    return pl.pallas_call(
-        functools.partial(total_kernel, count, sizes),
-        out_shape=jax.ShapeDtypeStruct(x.shape, x.dtype),
-        in_specs=[VMEM],
-        out_specs=VMEM,
-        scratch_shapes=[
-            pltpu.VMEM((count - 1,) + x.shape[1:], x.dtype),
-            pltpu.VMEM(x.shape[1:], x.dtype),
-        ]
-        + sems
-        + [pltpu.SemaphoreType.DMA],
-        compiler_params=pltpu.CompilerParams(
-            collective_id=collective_id, has_side_effects=True
-        ),
-        name="proc_total",
     )(x)
 
 
@@ -226,7 +173,179 @@
         in_specs=[VMEM] * 4,
         out_specs=VMEM,
         name="spectra_grad",
-    )(harm, legendre, gp, gc), pack
+    )(harm, legendre, gp, gc)
+
+
+def spectral_kernel(
+    modes,
+    pack,
+    sizes,
+    var_count,
+    weight,
+    spectra_ref,
+    legendre_ref,
+    terms_ref,
+    banded_ref,
+    coeff_ref,
+    harm,
+    power,
+    parts,
+    acc,
+    outgoing,
+    narrow,
+    sa,
+    ra,
+    sb,
+    rb,
+    sc,
+    rc,
+    sd,
+    rd,
+):
+    procs = sizes["proc"]
+    group_count = sizes["loss"] * sizes["vars"]
+    me, team = rank("proc", sizes), rank("group", sizes)
+    peers = [lax.rem(me + k, procs) for k in range(1, procs)]
+    mates = [lax.rem(team + k, group_count) for k in range(1, group_count)]
+    greet(
+        [place("proc", peer, sizes) for peer in peers]
+        + [place("group", mate, sizes) for mate in mates]
+    )
+    half = 2 * var_count
+    each = var_count // procs
+
+    def copy(src, dst, send, recv, device):
+        return pltpu.make_async_remote_copy(
+            src_ref=src,
+            dst_ref=dst,
+            send_sem=send,
+            recv_sem=recv,
+            device_id=device,
+            device_id_type=MESH,
+        )
+
+    sums = [jnp.zeros((half, LDEG), F32) for _ in range(3)]
+    for m in range(modes):
+        value = jnp.dot(
+            spectra_ref[m], legendre_ref[m], precision=HIGHEST, preferred_element_type=F32
+        )
+        harm[m] = value
+        pred, true = value[:half], value[half:]
+        sums = [sums[0] + pred * pred, sums[1] + true * true, sums[2] + pred * true]
+    for i in range(3):
+        total = sums[i][:var_count] + sums[i][var_count:]
+        for p in range(procs):
+            power[p, i * each : (i + 1) * each] = total[p * each : (p + 1) * each]
+
+    sent = [
+        copy(power.at[peer], parts.at[k], sa.at[k], ra.at[k], place("proc", peer, sizes))
+        for k, peer in enumerate(peers)
+    ]
+    for made in sent:
+        made.start()
+    for made in sent:
+        made.wait()
+    total = power[me]
+    for k in range(procs - 1):
+        total = total + parts[k]
+    powers = [total[i * each : (i + 1) * each] for i in range(3)]
+    terms, pullback = jax.vjp(amse_terms, *powers)
+    grad_pred, _, grad_cross = pullback(jnp.full((each, LDEG), weight, F32))
+    acc[...] = jnp.concatenate([2.0 * grad_pred, grad_cross, terms], axis=0)
+    terms_ref[me] = acc[...]
+    sent = [
+        copy(acc, terms_ref.at[me], sb.at[k], rb.at[k], place("proc", peer, sizes))
+        for k, peer in enumerate(peers)
+    ]
+    for made in sent:
+        made.start()
+    for made in sent:
+        made.wait()
+    gp = jnp.concatenate([terms_ref[p, :each] for p in range(procs)] * 2, axis=0)
+    gc = jnp.concatenate([terms_ref[p, each : 2 * each] for p in range(procs)] * 2, axis=0)
+
+    for hi in range(modes // pack):
+        columns = []
+        for lo in range(pack):
+            value = harm[hi * pack + lo]
+            grad = gp * value[:half] + gc * value[half:]
+            columns.append(
+                lax.dot_general(
+                    legendre_ref[hi * pack + lo],
+                    grad,
+                    NT,
+                    precision=HIGHEST,
+                    preferred_element_type=F32,
+                )
+            )
+        block = jnp.concatenate(columns, axis=1)
+        outgoing[:, hi] = block.reshape(procs, block.shape[0] // procs, block.shape[1])
+    sent = [
+        copy(outgoing.at[peer], banded_ref.at[me], sc.at[k], rc.at[k], place("proc", peer, sizes))
+        for k, peer in enumerate(peers)
+    ]
+    for made in sent:
+        made.start()
+    banded_ref[me] = outgoing[me]
+
+    passed = []
+    for k in range(procs):
+        source = lax.rem(me + procs - k, procs)
+        if k > 0:
+            sent[k - 1].wait_recv()
+        value = banded_ref[source].astype(BF16)
+        narrow[source] = value
+        coeff_ref[0, source] = value
+        for j, mate in enumerate(mates):
+            passed.append(
+                copy(
+                    narrow.at[source],
+                    coeff_ref.at[j + 1, source],
+                    sd.at[k, j],
+                    rd.at[k, j],
+                    place("group", mate, sizes),
+                )
+            )
+            passed[-1].start()
+    for made in sent:
+        made.wait_send()
+    for made in passed:
+        made.wait()
+
+
+def spectral(spectra, legendre, sizes, weight, collective_id):
+    procs = sizes["proc"]
+    group_count = sizes["loss"] * sizes["vars"]
+    modes, rows, lats = spectra.shape
+    var_count = rows // 4
+    each = var_count // procs
+    pack = min(modes, max(1, 128 // (2 * var_count)))
+    block = (procs, modes // pack, lats // procs, pack * 2 * var_count)
+    dma = pltpu.SemaphoreType.DMA
+    return pl.pallas_call(
+        functools.partial(spectral_kernel, modes, pack, sizes, var_count, weight),
+        out_shape=(
+            jax.ShapeDtypeStruct((procs, 3 * each, LDEG), F32),
+            jax.ShapeDtypeStruct(block, F32),
+            jax.ShapeDtypeStruct((group_count,) + block, BF16),
+        ),
+        in_specs=[VMEM, VMEM],
+        out_specs=(VMEM, VMEM, VMEM),
+        scratch_shapes=[
+            pltpu.VMEM((modes, rows, LDEG), F32),
+            pltpu.VMEM((procs, 3 * each, LDEG), F32),
+            pltpu.VMEM((procs - 1, 3 * each, LDEG), F32),
+            pltpu.VMEM((3 * each, LDEG), F32),
+            pltpu.VMEM(block, F32),
+            pltpu.VMEM(block, BF16),
+        ]
+        + [dma((procs - 1,)) for _ in range(6)]
+        + [dma((procs, group_count - 1)) for _ in range(2)],
+        compiler_params=pltpu.CompilerParams(
+            collective_id=collective_id, has_side_effects=True
+        ),
+        name="spectral",
+    )(spectra, legendre)
 
 
 def attention_kernel(
@@ -444,40 +563,39 @@
     width = head_local * HEAD
     share = model // group_count
 
-    to_modes = jnp.asarray(
-        basis.reshape(2, LON, procs, modes).transpose(2, 0, 3, 1).reshape(-1, LON), F32
-    )
+    ordered = basis.reshape(2, LON, procs, modes).transpose(2, 0, 3, 1).reshape(-1, LON)
+    to_modes = jnp.asarray(ordered, F32)
     fields = jnp.concatenate([prediction.astype(F32), target]).reshape(-1, LON)
     spectra = lax.dot_general(to_modes, fields, NT, precision=HIGHEST)
     at_owner = exchange(spectra.reshape(procs, 2 * modes, -1), "proc", sizes, 1)
     at_owner = at_owner.reshape(procs, 2, modes, 2, var_count, lats).transpose(2, 3, 1, 4, 0, 5)
-    harm, power = harmonics(at_owner.reshape(modes, 4 * var_count, lat_all), legendre)
-    if power.size % (procs * 128) == 0:
-        shaped = power.reshape(procs, -1, 128)
-        power = proc_total(shaped, sizes, 2).reshape(power.shape)
+    at_owner = at_owner.reshape(modes, 4 * var_count, lat_all)
+    weight_grad = lat_all * LON / (VARS * LDEG * modes_all)
+    if var_count % procs == 0:
+        terms, banded, coeff = spectral(at_owner, legendre, sizes, weight_grad, 2)
+        each = var_count // procs
+        degree_terms = terms[:, 2 * each :].reshape(var_count, LDEG)
     else:
+        harm, power = harmonics(at_owner, legendre)
         power = lax.psum(power, "proc")
-    degree_terms, pullback = jax.vjp(amse_terms, power[0], power[1], power[2])
+        degree_terms, pullback = jax.vjp(amse_terms, power[0], power[1], power[2])
+        grad_pred, _, grad_cross = pullback(jnp.full(degree_terms.shape, weight_grad, F32))
+        grad_spectra = spectra_grad(harm, legendre, grad_pred, grad_cross, procs)
+        banded = exchange(grad_spectra, "proc", sizes, 3)
+        coeff = exchange(banded.astype(BF16), "group", sizes, 4, spread=True)
     amse = jnp.sum(degree_terms, axis=-1) / (LDEG * modes_all)
-    weight_grad = lat_all * LON / (VARS * LDEG * modes_all)
-    grad_pred, _, grad_cross = pullback(jnp.full(degree_terms.shape, weight_grad, F32))
-    grad_spectra, pack = spectra_grad(harm, legendre, grad_pred, grad_cross, procs)
-    banded = exchange(grad_spectra, "proc", sizes, 3)
-    banded = banded.reshape(procs, modes // pack, lats, pack, 2, var_count)
-    banded = banded.transpose(0, 1, 3, 4, 5, 2).reshape(2 * modes_all, var_count, lats)
+    high, pack = banded.shape[1], modes // banded.shape[1]
+    banded = banded.reshape(procs, high, lats, pack, 2, var_count)
+    banded = banded.transpose(0, 4, 1, 3, 5, 2).reshape(2 * modes_all, var_count, lats)
 
     pairs = row_count // WR
-    sent = banded.astype(BF16).reshape(2 * modes_all, var_count, pairs, WR, 4)
-    sent = sent.transpose(0, 2, 3, 1, 4).reshape(2 * modes_all, -1)
-    coeff = exchange(sent, "group", sizes, 4, spread=True)
-    coeff = coeff.reshape(group_count, 2 * modes_all, pairs, WR, 4 * var_count)
-    coeff = coeff.transpose(2, 1, 3, 0, 4).reshape(pairs, 2 * modes_all, -1)
-
-    by_mode = basis.transpose(1, 2, 0).reshape(LON, 2 * modes_all)
+    coeff = coeff.reshape(group_count, procs, high, pairs, WR, 4, pack, 2, var_count)
+    coeff = coeff.transpose(3, 1, 7, 2, 6, 4, 0, 8, 5).reshape(pairs, 2 * modes_all, -1)
+
     field_grad = lax.dot_general(
         banded.reshape(2 * modes_all, -1),
-        jnp.asarray(by_mode, F32),
-        (((0,), (1,)), ((), ())),
+        to_modes,
+        (((0,), (0,)), ((), ())),
         precision=HIGHEST,
     ).reshape(var_count, lats, LON)
 
@@ -515,9 +633,7 @@
     projected = jnp.einsum(
         "brd,dk->brk", norm_out, w_flat, preferred_element_type=F32
     ).astype(BF16)
-    by_column = jnp.asarray(
-        by_mode.reshape(col_count, 4, 2 * modes_all).transpose(1, 0, 2), BF16
-    )
+    by_column = jnp.asarray(ordered.T.reshape(col_count, 4, -1).transpose(1, 0, 2), BF16)
     f_rolled = jnp.roll(by_column, -offset, axis=1)
     summed = attention_backward(
         f_rolled, coeff, mix, projected, rolled, ln_gain.reshape(1, model), w_flat, sizes, 6

time: 158 us -> 181 us (1.15)
  local copies, waits for them, and re-layouts: 46.9 us -> 80.4 us
  Pallas kernels: 80.3 us -> 70 us
    reshape x9 -> x7, local copies, waits for them, and re-layouts: 9.96 us -> 44.4 us  [the longest x2 18.6 us: body(): coeff.reshape(group_count, procs, high, pairs, WR, 4, pack, 2, var_count)]
    pallas_call x3 -> x1, Pallas kernels: 25.3 us -> 11.9 us  [exchange(): pl.pallas_call(functools.partial(exchange_kernel, axis, count, sizes, spr...]
    pallas_call x3 -> x1, Pallas kernels: 23.6 us -> 27.2 us  [spectral(): pl.pallas_call(functools.partial(spectral_kernel, modes, pack, sizes, var...]
    transpose x3 -> x0, local copies, waits for them, and re-layouts: 2.82 us -> none  [the longest x1 1.84 us: body(): banded.transpose(0, 1, 3, 4, 5, 2).reshape(2 * modes_all, var_count, lats)]
    unnamed x23 -> x27, local copies, waits for them, and re-layouts: 4.8 us -> 5.47 us
  transfers between devices with their start and end apart: 3 -> 3, of which waited for: 0 -> 0; matrix products, arithmetic and copies ran while one was open for 34% -> 48% of each run, Pallas kernels for 31% -> 22%
where the time goes in v2:
time: 181 us; the launch traced here: 180 us
  local copies, waits for them, and re-layouts  80.4 us (44%)
  Pallas kernels  70 us (39%)
  matrix products  15.6 us (9%)
  other arithmetic  9.3 us (5%)
  starting transfers between devices  3.2 us (2%)
    pallas_call x1, Pallas kernels, attention_backward(): pl.pallas_call(functools.partial(attention_kernel, heads, cols, blocks, s...  30.9 us
    pallas_call x1, Pallas kernels, spectral(): pl.pallas_call(functools.partial(spectral_kernel, modes, pack, sizes, var...  27.2 us
    reshape x2, local copies, waits for them, and re-layouts, body(): coeff.reshape(group_count, procs, high, pairs, WR, 4, pack, 2, var_count)  18.6 us
    reshape x1, local copies, waits for them, and re-layouts, body(): coeff.transpose(3, 1, 7, 2, 6, 4, 0, 8, 5).reshape(pairs, 2 * modes_all, -1)  17.6 us
    pallas_call x1, Pallas kernels, exchange(): pl.pallas_call(functools.partial(exchange_kernel, axis, count, sizes, spr...  11.9 us
    dot_general x1, matrix products, body(): jnp.einsum('brd,dk->brk', norm_out, w_flat, preferred_element_type=F32)  6.01 us
    unnamed x27, local copies, waits for them, and re-layouts  5.47 us
    transpose x1, local copies, waits for them, and re-layouts, body(): at_owner.reshape(procs, 2, modes, 2, var_count, lats)  5.26 us
  transfers between devices with their start and end apart: 3, of which 0 were waited for; matrix products, arithmetic and copies ran while one was open for 48% of the time, Pallas kernels for 22%

profile of v2, /device:TPU:0, one launch (start us, length us, event | category | flops | bytes accessed | tf_op | source)
XLA Modules:
  0.0 180.1 jit_solution(6422774487806140565)
XLA Ops:
  0.6 1.4 copy.36
  2.1 0.2 reshape.117
  2.3 0.3 reshape_reshape.7
  2.6 3.8 %convolution_convert_fusion.1 = bf16[256,1536]{1,0:T(8,128)(2,1)S(1)} fusion(bf16[256,1536]{1,0:T(8,128)(2,1)S(1)} %reshape.117, bf16[1536,1536]{1,0:T(8,128)(2,1)} %bitcast.80), kind=kOutput, calls=%fused_computation.10 | convolution fusion | flops 1208352768 | bytes 6291456 | tf_op jit(solution)/shard_map/dot_general | solution.py:603
  6.3 0.2 reshape.119
  6.5 0.3 constant_dynamic-update-slice_fusion.1
  6.8 0.4 constant_dynamic-update-slice_fusion
  7.2 4.0 %constant_dynamic-slice_fusion.3 = (bf16[256,1,768]{2,1,0:T(2,128)(2,1)}, bf16[256,1,768]{2,1,0:T(2,128)(2,1)S(1)}, bf16[256,1,768]{2,1,0:T(2,128)(2,1)S(1)}, bf16[256,1,768]{2,1,0:T(2,128)(2,1)S(1)}) fusion(bf16[256,4,768]{2,1,0:T(4,128)(2,1)S(1)} %constant_dynamic-update-slice_fusion, s32[]{:T(128)S(6)} %select_n.44, s32[]{:T(128)S(6)} %select_n.47, ...), kind=kLoop, calls=%fused_computation.33 | loop fusion | bytes 3145744 | tf_op jit(solution)/shard_map/dynamic-slice
  11.2 0.8 copy.50
  12.0 2.4 %collective-permute-start.2 = (bf16[256,768]{1,0:T(8,128)(2,1)}, bf16[256,768]{1,0:T(8,128)(2,1)}, u32[]{:S(2)}, u32[]{:S(2)}) collective-permute-start(bf16[256,768]{1,0:T(8,128)(2,1)} %bitcast.59), channel_id=1, source_target_pairs={{0,3},{1,0},{2,1},{3,2},{4,7},{5,4},{6,5},{7,6},{8,11},{9,8},{10,9... | collective-permute-start | bytes 1179656 | tf_op jit(solution)/shard_map/ppermute | solution.py:618
  14.4 0.8 copy.51
  15.2 0.6 collective-permute-start.1
  15.8 0.8 copy.52
  16.6 0.2 collective-permute-start
  17.5 3.4 %fusion.5 = bf16[2,360,1536]{2,1,0:T(8,128)(2,1)S(1)} fusion(s32[]{:T(128)S(6)} %select_n.43, bf16[2,360,1536]{2,1,0:T(8,128)(2,1)} %param.11), kind=kLoop, calls=%fused_computation.11 | loop fusion | flops 4423680 | bytes 4423684 | tf_op jit(solution)/shard_map/jit(_roll_dynamic)/concatenate | solution.py:625
  20.9 0.4 convert_reduce_fusion
  21.3 0.0 copy-start.7
  21.3 0.0 copy-start.4
  21.3 0.0 copy-start.5
  21.4 1.6 copy.40
  23.0 0.0 copy-done.7
  23.0 0.1 convert_element_type.21
  23.1 0.5 copy-done.4
  23.6 0.3 copy-done.5
  23.8 3.5 %fusion.6 = f32[256,256]{1,0:T(8,128)} fusion(f32[256,1440]{0,1:T(8,128)S(1)} %copy-done.4, f32[16,8,1440]{2,1,0:T(8,128)S(1)} %copy-done.5, f32[16,8,1440]{2,1,0:T(8,128)S(1)} %convert_element_type.21), kind=kOutput, calls=%fused_computation.13 | convolution fusion | flops 1132830720 | bytes 3211264 | tf_op jit(solution)/shard_map/dot_general | solution.py:569
  27.3 11.9 %exchange_1.1 = f32[8,32,256]{2,1,0:T(8,128)} custom-call(f32[8,32,256]{2,1,0:T(8,128)} %bitcast.77), custom_call_target="tpu_custom_call" | custom-call | tf_op jit(solution)/shard_map/exchange_1/pallas_call | solution.py:98
  39.3 1.3 copy.30
  40.6 2.5 %reshape.112 = f32[8,2,16,2,16,8]{2,1,5,4,3,0:T(2,128)} reshape(f32[8,32,256]{1,2,0:T(8,128)S(1)} %copy.30) | data formatting | bytes 524288 | tf_op jit(solution)/shard_map/reshape | solution.py:571
  43.1 5.3 %copy.31 = f32[16,2,2,16,8,8]{3,2,1,5,4,0:T(2,128)} copy(f32[16,2,2,16,8,8]{0,2,5,3,1,4:T(2,128)} %bitcast.68) | data formatting | bytes 524288 | tf_op jit(solution)/shard_map/transpose | solution.py:571
  48.4 3.1 %reshape.113 = f32[16,64,64]{1,2,0:T(8,128)S(1)} reshape(f32[16,2,2,16,8,8]{3,2,1,5,4,0:T(2,128)} %copy.31) | data formatting | bytes 524288 | tf_op jit(solution)/shard_map/reshape | solution.py:572
  51.5 1.0 copy.32.spectra_ref
  52.5 27.2 %spectral.1 = (f32[8,6,384]{2,1,0:T(8,128)}, f32[8,4,8,128]{3,2,1,0:T(8,128)}, bf16[4,8,4,8,128]{4,3,2,1,0:T(8,128)(2,1)}) custom-call(f32[16,64,64]{2,1,0:T(8,128)} %copy.32.spectra_ref, f32[16,64,384]{2,1,0:T(8,128)} %legendre_ref.1), custom_call_target="tpu_custom_call" | custom-call | tf_op jit(solution)/shard_map/spectral/pallas_call | solution.py:325
  79.7 1.0 slice_reduce_fusion
  80.7 0.6 div.12
  81.3 2.2 %reshape.114 = f32[8,4,8,4,2,16]{5,4,3,2,1,0:T(2,128)S(1)} reshape(f32[8,4,8,128]{3,2,1,0:T(8,128)} %get-tuple-element.7) | data formatting | bytes 262144 | tf_op jit(solution)/shard_map/reshape | solution.py:588
  83.5 0.0 copy-start.9
  83.5 1.9 %copy.33 = f32[8,4,8,4,2,16]{2,5,3,1,4,0:T(8,128)} copy(f32[8,4,8,4,2,16]{5,4,3,2,1,0:T(2,128)S(1)} %reshape.114) | data formatting | bytes 262144 | tf_op jit(solution)/shard_map/reshape | solution.py:588
  85.4 2.6 %reshape_reshape.6 = f32[256,128]{1,0:T(8,128)S(1)} reshape(f32[8,2,4,4,16,8]{5,4,3,2,1,0:T(8,128)} %bitcast.69) | data formatting | bytes 262144 | tf_op jit(solution)/shard_map/reshape;reshape | solution.py:596
  88.1 0.8 copy.34
  88.8 0.0 copy-done.9
  88.8 2.3 %reshape.115 = bf16[4,8,4,1,2,4,4,2,16]{8,7,6,5,4,2,1,0,3:T(2,128)(2,1)} reshape(bf16[4,8,4,8,128]{4,3,2,1,0:T(8,128)(2,1)S(1)} %copy-done.9) | data formatting | bytes 524288 | tf_op jit(solution)/shard_map/reshape | solution.py:592
  91.2 16.2 %copy.35 = bf16[4,8,4,1,2,4,4,2,16]{5,8,0,4,6,2,7,1,3:T(8,128)(2,1)} copy(bf16[4,8,4,1,2,4,4,2,16]{8,7,6,5,4,2,1,0,3:T(2,128)(2,1)} %reshape.115) | data formatting | bytes 524288 | tf_op jit(solution)/shard_map/reshape | solution.py:592
  107.4 17.6 %reshape.116.coeff_ref = bf16[1,256,512]{2,1,0:T(8,128)(2,1)} reshape(bf16[1,8,2,4,4,2,4,16,4]{8,7,6,5,4,3,2,1,0:T(8,128)(2,1)} %bitcast.66) | data formatting | bytes 524288 | tf_op jit(solution)/shard_map/reshape | solution.py:593
  125.0 0.8 copy.43
  125.8 0.7 fusion.2
  126.6 0.6 reshape.124.gain_ref
  127.1 0.7 fusion.4
  127.9 0.0 copy-start
  127.9 1.6 copy.39
  129.5 1.2 copy-done
  130.7 3.8 %copy.41.w_ref = bf16[1536,1152]{1,0:T(8,128)(2,1)} copy(bf16[1536,1152]{0,1:T(8,128)(2,1)S(1)} %bitcast.71) | data formatting | bytes 7077888 | tf_op jit(solution)/shard_map/reshape | solution.py:632
  134.4 6.0 %convolution_convert_fusion.proj_ref = bf16[5,144,1152]{2,1,0:T(8,128)(2,1)} fusion(bf16[5,144,1536]{2,1,0:T(8,128)(2,1)} %bitcast.73, bf16[1536,1152,1]{0,1,2:T(8,128)(2,1)S(1)} %bitcast.72), kind=kOutput, calls=%fused_computation.9 | convolution fusion | flops 2548869120 | bytes 7409664 | tf_op jit(solution)/shard_map/brd,dk->brk/dot_general | solution.py:633
  140.5 1.0 constant_dynamic-slice_fusion.4.f_ref
  141.5 0.0 copy-done.3
  141.5 2.4 %fusion.10 = f32[16,8,1440]{2,1,0:T(8,128)} fusion(f32[256,1440,1]{0,1,2:T(8,128)S(1)} %copy-done.3, f32[128,256]{1,0:T(8,128)S(1)} %copy-done.6), kind=kOutput, calls=%fused_computation.23 | convolution fusion | flops 566231040 | bytes 2342912 | tf_op jit(solution)/shard_map/dot_general | solution.py:595
  143.9 0.0 collective-permute-done.2
  143.9 0.0 collective-permute-done.1
  143.9 0.0 collective-permute-done
  143.9 0.0 copy-done.2
  143.9 1.4 maximum_bitcast_fusion.2
  145.3 1.3 copy.38
  146.6 30.9 %attention_backward.1 = bf16[5,144,384]{2,1,0:T(8,128)(2,1)} custom-call(bf16[4,360,256]{2,1,0:T(8,128)(2,1)} %constant_dynamic-slice_fusion.4.f_ref, bf16[1,256,512]{2,1,0:T(8,128)(2,1)} %reshape.116.coeff_ref, bf16[1024,768]{1,0:T(8,128)(2,1)} %bitcast.70, bf16[5,144,1152]{2,1,0:T(8,128)(2,1)} %convolution_convert_fusion.proj_ref, ...), custom_call_target="tpu_custom_call" | custom-call | tf_op jit(solution)/shard_map/attention_backward/pallas_call | solution.py:518
  177.5 1.1 copy.42
  178.6 1.5 fusion.9
  (13 shorter events, 0.0 us)
Async XLA Ops:
  12.0 131.9 %collective-permute-start.2 = (bf16[256,768]{1,0:T(8,128)(2,1)}, bf16[256,768]{1,0:T(8,128)(2,1)}, u32[]{:S(2)}, u32[]{:S(2)}) collective-permute-start(bf16[256,768]{1,0:T(8,128)(2,1)} %bitcast.59), channel_id=1, source_target_pairs={{0,3},{1,0},{2,1},{3,2},{4,7},{5,4},{6,5},{7,6},{8,11},{9,8},{10,9... | collective-permute-start | bytes 1179656 | tf_op jit(solution)/shard_map/ppermute | solution.py:618
  15.2 128.7 %collective-permute-start.1 = (bf16[256,768]{1,0:T(8,128)(2,1)}, bf16[256,768]{1,0:T(8,128)(2,1)}, u32[]{:S(2)}, u32[]{:S(2)}) collective-permute-start(bf16[256,768]{1,0:T(8,128)(2,1)} %bitcast.60), channel_id=1, source_target_pairs={{0,2},{1,3},{2,0},{3,1},{4,6},{5,7},{6,4},{7,5},{8,10},{9,11},{10,... | collective-permute-start | bytes 1179656 | tf_op jit(solution)/shard_map/ppermute | solution.py:618
  16.6 127.3 %collective-permute-start = (bf16[256,768]{1,0:T(8,128)(2,1)}, bf16[256,768]{1,0:T(8,128)(2,1)}, u32[]{:S(2)}, u32[]{:S(2)}) collective-permute-start(bf16[256,768]{1,0:T(8,128)(2,1)} %bitcast.61), channel_id=1, source_target_pairs={{0,1},{1,2},{2,3},{3,0},{4,5},{5,6},{6,7},{7,4},{8,9},{9,10},{10,1... | collective-permute-start | bytes 1179656 | tf_op jit(solution)/shard_map/ppermute | solution.py:618
  21.3 1.7 copy-start.7
  21.3 2.2 %copy-start.4 = (f32[256,1440]{0,1:T(8,128)S(1)}, f32[256,1440]{0,1:T(8,128)}, u32[]{:S(2)}) copy-start(f32[256,1440]{0,1:T(8,128)} %constant.88.clone) | copy-start | bytes 4423684
  21.3 2.5 %copy-start.5 = (f32[16,8,1440]{2,1,0:T(8,128)S(1)}, f32[16,8,1440]{2,1,0:T(8,128)}, u32[]{:S(2)}) copy-start(f32[16,8,1440]{2,1,0:T(8,128)} %param.18) | copy-start | bytes 2211844
  83.5 5.3 %copy-start.9 = (bf16[4,8,4,8,128]{4,3,2,1,0:T(8,128)(2,1)S(1)}, bf16[4,8,4,8,128]{4,3,2,1,0:T(8,128)(2,1)}, u32[]{:S(2)}) copy-start(bf16[4,8,4,8,128]{4,3,2,1,0:T(8,128)(2,1)} %get-tuple-element.8) | copy-start | bytes 786436
  107.4 17.6 %copy-start.1 = (bf16[256,1,768]{2,1,0:T(2,128)(2,1)S(1)}, bf16[256,1,768]{2,1,0:T(2,128)(2,1)}, u32[]{:S(2)}) copy-start(bf16[256,1,768]{2,1,0:T(2,128)(2,1)} %get-tuple-element.9) | copy-start | bytes 1179652
  125.0 1.6 copy-start.10
  127.9 2.8 %copy-start = (bf16[1536,3,4,96]{0,3,2,1:T(8,128)(2,1)S(1)}, bf16[1536,3,4,96]{0,3,2,1:T(8,128)(2,1)}, u32[]{:S(2)}) copy-start(bf16[1536,3,4,96]{0,3,2,1:T(8,128)(2,1)} %param.13) | copy-start | bytes 10616836
  134.4 6.0 %copy-start.8 = (bf16[4,720,256]{2,1,0:T(8,128)(2,1)S(1)}, bf16[4,720,256]{2,1,0:T(8,128)(2,1)}, u32[]{:S(2)}) copy-start(bf16[4,720,256]{2,1,0:T(8,128)(2,1)} %constant.91) | copy-start | bytes 4423684
  134.4 7.1 %copy-start.3 = (f32[256,1440,1]{0,1,2:T(8,128)S(1)}, f32[256,1440,1]{0,1,2:T(8,128)}, u32[]{:S(2)}) copy-start(f32[256,1440,1]{0,1,2:T(8,128)} %constant.92) | copy-start | bytes 4423684
  134.4 7.1 %copy-start.6 = (f32[128,256]{1,0:T(8,128)S(1)}, f32[128,256]{1,0:T(8,128)}, u32[]{:S(2)}) copy-start(f32[128,256]{1,0:T(8,128)} %copy.34) | copy-start | bytes 393220
  140.5 3.4 %copy-start.2 = (bf16[256,1,768]{2,0,1:T(8,128)(2,1)S(1)}, bf16[256,1,768]{2,0,1:T(8,128)(2,1)}, u32[]{:S(2)}) copy-start(bf16[256,1,768]{2,0,1:T(8,128)(2,1)} %copy.43) | copy-start | bytes 1179652

commit v3 on v2

--- a/solution.py
+++ b/solution.py
@@ -141,44 +141,8 @@
     )(spectra, legendre)
 
 
-def spectra_grad_kernel(modes, pack, procs, var_count, harm_ref, legendre_ref, gp_ref, gc_ref, out_ref):
-    half = 2 * var_count
-    gp = jnp.concatenate([gp_ref[...], gp_ref[...]], axis=0) * 2.0
-    gc = jnp.concatenate([gc_ref[...], gc_ref[...]], axis=0)
-    for hi in range(modes // pack):
-        columns = []
-        for lo in range(pack):
-            m = hi * pack + lo
-            harm = harm_ref[m]
-            grad = gp * harm[:half] + gc * harm[half:]
-            columns.append(
-                lax.dot_general(
-                    legendre_ref[m], grad, NT, precision=HIGHEST, preferred_element_type=F32
-                )
-            )
-        block = jnp.concatenate(columns, axis=1)
-        out_ref[:, hi] = block.reshape(procs, block.shape[0] // procs, block.shape[1])
-
-
-def spectra_grad(harm, legendre, gp, gc, procs):
-    modes, rows, _ = harm.shape
-    lats = legendre.shape[1]
-    var_count = rows // 4
-    pack = min(modes, max(1, 128 // (2 * var_count)))
-    return pl.pallas_call(
-        functools.partial(spectra_grad_kernel, modes, pack, procs, var_count),
-        out_shape=jax.ShapeDtypeStruct(
-            (procs, modes // pack, lats // procs, pack * 2 * var_count), F32
-        ),
-        in_specs=[VMEM] * 4,
-        out_specs=VMEM,
-        name="spectra_grad",
-    )(harm, legendre, gp, gc)
-
-
 def spectral_kernel(
     modes,
-    pack,
     sizes,
     var_count,
     weight,
@@ -191,6 +155,7 @@
     power,
     parts,
     acc,
+    rows,
     outgoing,
     narrow,
     sa,
@@ -264,22 +229,24 @@
     gp = jnp.concatenate([terms_ref[p, :each] for p in range(procs)] * 2, axis=0)
     gc = jnp.concatenate([terms_ref[p, each : 2 * each] for p in range(procs)] * 2, axis=0)
 
-    for hi in range(modes // pack):
-        columns = []
-        for lo in range(pack):
-            value = harm[hi * pack + lo]
-            grad = gp * value[:half] + gc * value[half:]
-            columns.append(
-                lax.dot_general(
-                    legendre_ref[hi * pack + lo],
-                    grad,
-                    NT,
-                    precision=HIGHEST,
-                    preferred_element_type=F32,
-                )
-            )
-        block = jnp.concatenate(columns, axis=1)
-        outgoing[:, hi] = block.reshape(procs, block.shape[0] // procs, block.shape[1])
+    lats = legendre_ref.shape[1]
+    own = lats // procs
+    for m in range(modes):
+        value = harm[m]
+        grad = gp * value[:half] + gc * value[half:]
+        rows[m * half : (m + 1) * half, :lats] = lax.dot_general(
+            grad, legendre_ref[m], NT, precision=HIGHEST, preferred_element_type=F32
+        )
+    by_var = [rows[pl.ds(v, 2 * modes, stride=var_count), :] for v in range(var_count)]
+    for q in range(procs):
+        outgoing[q] = jnp.concatenate(
+            [
+                by_var[v][:, q * own + 4 * r : q * own + 4 * r + 4]
+                for r in range(own // 4)
+                for v in range(var_count)
+            ],
+            axis=1,
+        )
     sent = [
         copy(outgoing.at[peer], banded_ref.at[me], sc.at[k], rc.at[k], place("proc", peer, sizes))
         for k, peer in enumerate(peers)
@@ -319,11 +286,10 @@
     modes, rows, lats = spectra.shape
     var_count = rows // 4
     each = var_count // procs
-    pack = min(modes, max(1, 128 // (2 * var_count)))
-    block = (procs, modes // pack, lats // procs, pack * 2 * var_count)
+    block = (procs, 2 * modes, var_count * lats // procs)
     dma = pltpu.SemaphoreType.DMA
     return pl.pallas_call(
-        functools.partial(spectral_kernel, modes, pack, sizes, var_count, weight),
+        functools.partial(spectral_kernel, modes, sizes, var_count, weight),
         out_shape=(
             jax.ShapeDtypeStruct((procs, 3 * each, LDEG), F32),
             jax.ShapeDtypeStruct(block, F32),
@@ -336,6 +302,7 @@
             pltpu.VMEM((procs, 3 * each, LDEG), F32),
             pltpu.VMEM((procs - 1, 3 * each, LDEG), F32),
             pltpu.VMEM((3 * each, LDEG), F32),
+            pltpu.VMEM((2 * modes * var_count, pl.cdiv(lats, 128) * 128), F32),
             pltpu.VMEM(block, F32),
             pltpu.VMEM(block, BF16),
         ]
@@ -563,12 +530,12 @@
     width = head_local * HEAD
     share = model // group_count
 
-    ordered = basis.reshape(2, LON, procs, modes).transpose(2, 0, 3, 1).reshape(-1, LON)
+    ordered = basis.transpose(2, 0, 1).reshape(-1, LON)
     to_modes = jnp.asarray(ordered, F32)
     fields = jnp.concatenate([prediction.astype(F32), target]).reshape(-1, LON)
     spectra = lax.dot_general(to_modes, fields, NT, precision=HIGHEST)
     at_owner = exchange(spectra.reshape(procs, 2 * modes, -1), "proc", sizes, 1)
-    at_owner = at_owner.reshape(procs, 2, modes, 2, var_count, lats).transpose(2, 3, 1, 4, 0, 5)
+    at_owner = at_owner.reshape(procs, modes, 2, 2, var_count, lats).transpose(1, 3, 2, 4, 0, 5)
     at_owner = at_owner.reshape(modes, 4 * var_count, lat_all)
     weight_grad = lat_all * LON / (VARS * LDEG * modes_all)
     if var_count % procs == 0:
@@ -580,17 +547,18 @@
         power = lax.psum(power, "proc")
         degree_terms, pullback = jax.vjp(amse_terms, power[0], power[1], power[2])
         grad_pred, _, grad_cross = pullback(jnp.full(degree_terms.shape, weight_grad, F32))
-        grad_spectra = spectra_grad(harm, legendre, grad_pred, grad_cross, procs)
+        harm = harm.reshape(modes, 2, 2, var_count, LDEG)
+        grad_harm = 2.0 * grad_pred * harm[:, 0] + grad_cross * harm[:, 1]
+        grad_spectra = jnp.einsum("mcvl,mal->mcva", grad_harm, legendre, precision=HIGHEST)
+        grad_spectra = grad_spectra.reshape(modes, 2, var_count, procs, lats // 4, 4)
+        grad_spectra = grad_spectra.transpose(3, 0, 1, 4, 2, 5).reshape(procs, 2 * modes, -1)
         banded = exchange(grad_spectra, "proc", sizes, 3)
         coeff = exchange(banded.astype(BF16), "group", sizes, 4, spread=True)
     amse = jnp.sum(degree_terms, axis=-1) / (LDEG * modes_all)
-    high, pack = banded.shape[1], modes // banded.shape[1]
-    banded = banded.reshape(procs, high, lats, pack, 2, var_count)
-    banded = banded.transpose(0, 4, 1, 3, 5, 2).reshape(2 * modes_all, var_count, lats)
-
     pairs = row_count // WR
-    coeff = coeff.reshape(group_count, procs, high, pairs, WR, 4, pack, 2, var_count)
-    coeff = coeff.transpose(3, 1, 7, 2, 6, 4, 0, 8, 5).reshape(pairs, 2 * modes_all, -1)
+    banded = banded.reshape(2 * modes_all, row_count, var_count, 4).transpose(0, 2, 1, 3)
+    coeff = coeff.reshape(group_count, 2 * modes_all, pairs, WR, 4 * var_count)
+    coeff = coeff.transpose(2, 1, 3, 0, 4).reshape(pairs, 2 * modes_all, -1)
 
     field_grad = lax.dot_general(
         banded.reshape(2 * modes_all, -1),
@@ -620,7 +588,7 @@
     mix = mix.reshape(group_count, 4, 4 * var_count, width + share).transpose(1, 0, 2, 3)
     mix = mix.reshape(-1, width + share)
 
-    cols = 72
+    cols = 120
     split = (pairs, WR, col_count // cols, cols)
     rolled = jnp.roll(tokens, -offset, axis=1)
     rolled = rolled.reshape(split + (model,)).transpose(0, 2, 1, 3, 4)

time: 181 us -> 142 us (0.78)
  local copies, waits for them, and re-layouts: 80.4 us -> 44.1 us
  Pallas kernels: 70 us -> 67.8 us
    reshape x6 -> x5, local copies, waits for them, and re-layouts: 42.8 us -> 9.17 us  [the longest x1 4.62 us: body(): at_owner.reshape(procs, modes, 2, 2, var_count, lats)]
    another operation x2 -> x1, local copies, waits for them, and re-layouts: 6.68 us -> 3.3 us
    pallas_call x1, Pallas kernels: 30.9 us -> 27.8 us  [attention_backward(): pl.pallas_call(functools.partial(attention_kernel, heads, cols, blocks, s...]
    transpose x1 -> x3, local copies, waits for them, and re-layouts: 5.26 us -> 6.82 us  [the longest x1 4.88 us: body(): at_owner.reshape(procs, modes, 2, 2, var_count, lats)]
    unnamed x27 -> x23, local copies, waits for them, and re-layouts: 5.47 us -> 5.54 us
  transfers between devices with their start and end apart: 3 -> 3, of which waited for: 0 -> 0; matrix products, arithmetic and copies ran while one was open for 48% -> 36% of each run, Pallas kernels for 22% -> 28%
where the time goes in v3:
time: 142 us
  Pallas kernels  67.8 us (48%)
  local copies, waits for them, and re-layouts  44.1 us (31%)
  matrix products  15.7 us (11%)
  other arithmetic  9.24 us (7%)
  starting transfers between devices  3.2 us (2%)
  between operations  1.58 us (1%)
    pallas_call x1, Pallas kernels, spectral(): pl.pallas_call(functools.partial(spectral_kernel, modes, sizes, var_count...  28.1 us
    pallas_call x1, Pallas kernels, attention_backward(): pl.pallas_call(functools.partial(attention_kernel, heads, cols, blocks, s...  27.8 us
    pallas_call x1, Pallas kernels, exchange(): pl.pallas_call(functools.partial(exchange_kernel, axis, count, sizes, spr...  12 us
    dot_general x1, matrix products, body(): jnp.einsum('brd,dk->brk', norm_out, w_flat, preferred_element_type=F32)  6.05 us
    unnamed x23, local copies, waits for them, and re-layouts  5.54 us
    transpose x1, local copies, waits for them, and re-layouts, body(): at_owner.reshape(procs, modes, 2, 2, var_count, lats)  4.88 us
    reshape x1, local copies, waits for them, and re-layouts, body(): at_owner.reshape(procs, modes, 2, 2, var_count, lats)  4.62 us
    reshape x2, local copies, waits for them, and re-layouts, body(): at_owner = at_owner.reshape(modes, 4 * var_count, lat_all)  4.13 us
  transfers between devices with their start and end apart: 3, of which 0 were waited for; matrix products, arithmetic and copies ran while one was open for 36% of the time, Pallas kernels for 28%

profile of v3, /device:TPU:0, one launch (start us, length us, event | category | flops | bytes accessed | tf_op | source)
XLA Modules:
  0.0 141.6 jit_solution(5386371141639074664)
XLA Ops:
  0.6 1.4 %copy.35 = bf16[4,16,4,1536]{3,2,1,0:T(4,128)(2,1)S(1)} copy(bf16[4,16,4,1536]{3,0,2,1:T(4,128)(2,1)} %bitcast.76) | data formatting | bytes 1572864 | tf_op jit(solution)/shard_map/transpose | solution.py:570
  2.1 0.2 reshape.121
  2.3 0.3 reshape_reshape.3
  2.6 3.8 %convolution_convert_fusion.1 = bf16[256,1536]{1,0:T(8,128)(2,1)S(1)} fusion(bf16[256,1536]{1,0:T(8,128)(2,1)S(1)} %reshape.121, bf16[1536,1536]{1,0:T(8,128)(2,1)} %bitcast.78), kind=kOutput, calls=%fused_computation.10 | convolution fusion | flops 1208352768 | bytes 6291456 | tf_op jit(solution)/shard_map/dot_general | solution.py:571
  6.3 0.2 reshape.123
  6.5 0.3 constant_dynamic-update-slice_fusion.1
  6.8 0.4 constant_dynamic-update-slice_fusion
  7.2 3.3 %constant_dynamic-slice_fusion.3 = (bf16[256,1,768]{2,1,0:T(2,128)(2,1)S(1)}, bf16[256,1,768]{2,1,0:T(2,128)(2,1)S(1)}, bf16[256,1,768]{2,1,0:T(2,128)(2,1)S(1)}, bf16[256,1,768]{2,1,0:T(2,128)(2,1)S(1)}) fusion(bf16[256,4,768]{2,1,0:T(4,128)(2,1)S(1)} %constant_dynamic-update-slice_fusion, s32[]{:T(128)S(6)} %select_n.44, s32[]{:T(128)S(6)} %select_n.47, ...), kind=kLoop, calls=%fused_computation.32 | loop fusion | bytes 3145744 | tf_op jit(solution)/shard_map/dynamic-slice
  10.5 0.8 copy.50
  11.3 2.4 %collective-permute-start.2 = (bf16[256,768]{1,0:T(8,128)(2,1)}, bf16[256,768]{1,0:T(8,128)(2,1)}, u32[]{:S(2)}, u32[]{:S(2)}) collective-permute-start(bf16[256,768]{1,0:T(8,128)(2,1)} %bitcast.57), channel_id=1, source_target_pairs={{0,3},{1,0},{2,1},{3,2},{4,7},{5,4},{6,5},{7,6},{8,11},{9,8},{10,9... | collective-permute-start | bytes 1179656 | tf_op jit(solution)/shard_map/ppermute | solution.py:586
  13.7 0.8 copy.51
  14.5 0.6 collective-permute-start.1
  15.1 0.8 copy.52
  15.8 0.2 collective-permute-start
  16.8 3.4 %fusion.5 = bf16[2,360,1536]{2,1,0:T(8,128)(2,1)S(1)} fusion(s32[]{:T(128)S(6)} %select_n.43, bf16[2,360,1536]{2,1,0:T(8,128)(2,1)} %param.11), kind=kLoop, calls=%fused_computation.11 | loop fusion | flops 4423680 | bytes 4423684 | tf_op jit(solution)/shard_map/jit(_roll_dynamic)/concatenate | solution.py:593
  20.2 0.4 convert_reduce_fusion
  20.5 0.0 copy-start.6
  20.6 0.0 copy-start.3
  20.6 0.0 copy-start.4
  20.6 1.6 %copy.39 = bf16[1,3,2,120,1536]{4,3,2,1,0:T(8,128)(2,1)} copy(bf16[1,3,2,120,1536]{4,3,1,2,0:T(8,128)(2,1)S(1)} %bitcast.61) | data formatting | bytes 4423680 | tf_op jit(solution)/shard_map/transpose | solution.py:594
  22.2 0.0 copy-done.6
  22.2 0.1 convert_element_type.21
  22.3 0.5 copy-done.3
  22.8 0.3 copy-done.4
  23.1 3.5 %fusion.6 = f32[256,256]{1,0:T(8,128)} fusion(f32[256,1440]{0,1:T(8,128)S(1)} %copy-done.3, f32[16,8,1440]{2,1,0:T(8,128)S(1)} %copy-done.4, f32[16,8,1440]{2,1,0:T(8,128)S(1)} %convert_element_type.21), kind=kOutput, calls=%fused_computation.13 | convolution fusion | flops 1132830720 | bytes 3211264 | tf_op jit(solution)/shard_map/dot_general | solution.py:536
  26.6 12.0 %exchange_1.1 = f32[8,32,256]{2,1,0:T(8,128)} custom-call(f32[8,32,256]{2,1,0:T(8,128)} %bitcast.74), custom_call_target="tpu_custom_call" | custom-call | tf_op jit(solution)/shard_map/exchange_1/pallas_call | solution.py:98
  38.5 4.6 %reshape.115 = f32[8,16,2,2,16,8]{5,4,3,2,1,0:T(8,128)} reshape(f32[8,32,256]{2,1,0:T(8,128)} %exchange_1.1) | data formatting | bytes 524288 | tf_op jit(solution)/shard_map/reshape | solution.py:538
  43.1 4.9 %copy.30 = f32[16,2,2,16,8,8]{3,2,1,5,4,0:T(2,128)} copy(f32[16,2,2,16,8,8]{5,3,1,2,0,4:T(8,128)} %bitcast.64) | data formatting | bytes 524288 | tf_op jit(solution)/shard_map/transpose | solution.py:538
  48.0 3.1 %reshape.116 = f32[16,64,64]{1,2,0:T(8,128)S(1)} reshape(f32[16,2,2,16,8,8]{3,2,1,5,4,0:T(2,128)} %copy.30) | data formatting | bytes 524288 | tf_op jit(solution)/shard_map/reshape | solution.py:539
  51.2 1.0 copy.31.spectra_ref
  52.2 28.1 %spectral.1 = (f32[8,6,384]{2,1,0:T(8,128)}, f32[8,32,128]{2,1,0:T(8,128)}, bf16[4,8,32,128]{3,2,1,0:T(8,128)(2,1)}) custom-call(f32[16,64,64]{2,1,0:T(8,128)} %copy.31.spectra_ref, f32[16,64,384]{2,1,0:T(8,128)} %legendre_ref.1), custom_call_target="tpu_custom_call" | custom-call | tf_op jit(solution)/shard_map/spectral/pallas_call | solution.py:291
  80.2 1.0 slice_reduce_fusion
  81.2 0.6 div.12
  81.8 1.1 copy.32
  83.0 0.9 reshape.117
  83.8 0.9 copy.33
  84.8 0.7 reshape.118
  85.5 1.2 reshape.119
  86.7 0.0 copy-start.8
  86.7 1.0 copy.34
  87.7 1.8 %copy.40.coeff_ref = bf16[1,256,512]{2,1,0:T(8,128)(2,1)} copy(bf16[1,256,512]{1,2,0:T(8,128)(2,1)} %bitcast.75) | data formatting | bytes 524288 | tf_op jit(solution)/shard_map/reshape | solution.py:561
  89.5 0.8 copy.43
  90.3 0.7 fusion.2
  91.0 0.0 copy-done.8
  91.0 0.6 reshape.128.gain_ref
  91.6 0.7 fusion.4
  92.4 0.0 copy-start
  92.4 1.5 %copy.38 = bf16[1,3,2,120,1536]{4,3,2,1,0:T(8,128)(2,1)} copy(bf16[1,3,2,120,1536]{4,3,1,2,0:T(8,128)(2,1)S(1)} %fusion.4) | data formatting | bytes 4423680 | tf_op jit(solution)/shard_map/convert_element_type | solution.py:599
  93.9 1.3 copy-done
  95.2 3.8 %copy.41.w_ref = bf16[1536,1152]{1,0:T(8,128)(2,1)} copy(bf16[1536,1152]{0,1:T(8,128)(2,1)S(1)} %bitcast.67) | data formatting | bytes 7077888 | tf_op jit(solution)/shard_map/reshape | solution.py:600
  99.0 6.0 %convolution_convert_fusion.proj_ref = bf16[3,240,1152]{2,1,0:T(8,128)(2,1)} fusion(bf16[3,240,1536]{2,1,0:T(8,128)(2,1)} %bitcast.69, bf16[1536,1152,1]{0,1,2:T(8,128)(2,1)S(1)} %bitcast.68), kind=kOutput, calls=%fused_computation.9 | convolution fusion | flops 2548869120 | bytes 7409664 | tf_op jit(solution)/shard_map/brd,dk->brk/dot_general | solution.py:601
  105.0 0.0 copy-done.7
  105.0 1.1 constant_dynamic-slice_fusion.4.f_ref
  106.1 0.0 copy-done.2
  106.1 0.0 copy-done.5
  106.1 2.4 %fusion.10 = f32[16,8,1440]{2,1,0:T(8,128)} fusion(f32[256,1440,1]{0,1,2:T(8,128)S(1)} %copy-done.2, f32[256,128]{0,1:T(8,128)S(1)} %copy-done.5), kind=kOutput, calls=%fused_computation.23 | convolution fusion | flops 566231040 | bytes 2342912 | tf_op jit(solution)/shard_map/dot_general | solution.py:563
  108.4 0.0 collective-permute-done.2
  108.5 0.0 collective-permute-done.1
  108.5 0.0 collective-permute-done
  108.5 1.4 %maximum_bitcast_fusion.2 = bf16[4,4,64,768]{3,2,0,1:T(8,128)(2,1)S(1)} fusion(bf16[1,4,64,768]{3,2,1,0:T(8,128)(2,1)} %bitcast.14, bf16[1,4,64,768]{3,2,1,0:T(8,128)(2,1)} %bitcast.13, bf16[1,4,64,768]{3,2,1,0:T(8,128)(2,1)} %bitcast.12, bf16[1,4,64,768]{3,2,1,0:T(8,128)(2,1)S(1)} %bitcast.73), kind=kLoop, calls=%fused_computation.16 | loop fusion | flops 2359296 | bytes 3145728 | tf_op jit(solution)/shard_map/transpose | solution.py:588
  109.9 1.3 copy.37
  111.2 27.8 %attention_backward.1 = bf16[3,240,384]{2,1,0:T(8,128)(2,1)} custom-call(bf16[4,360,256]{2,1,0:T(8,128)(2,1)} %constant_dynamic-slice_fusion.4.f_ref, bf16[1,256,512]{2,1,0:T(8,128)(2,1)} %copy.40.coeff_ref, bf16[1024,768]{1,0:T(8,128)(2,1)} %bitcast.66, bf16[3,240,1152]{2,1,0:T(8,128)(2,1)} %convolution_convert_fusion.proj_ref, ...), custom_call_target="tpu_custom_call" | custom-call | tf_op jit(solution)/shard_map/attention_backward/pallas_call | solution.py:485
  139.0 1.1 copy.42
  140.1 1.5 %fusion.9 = bf16[2,360,384]{2,1,0:T(8,128)(2,1)} fusion(s32[]{:T(128)S(6)} %select_n.49, bf16[2,360,384]{2,1,0:T(8,128)(2,1)S(1)} %bitcast.70), kind=kLoop, calls=%fused_computation.19 | loop fusion | flops 1105920 | bytes 1105924 | tf_op jit(solution)/shard_map/jit(_roll_dynamic)/concatenate | solution.py:610
  (8 shorter events, 0.0 us)
Async XLA Ops:
  11.3 97.2 %collective-permute-start.2 = (bf16[256,768]{1,0:T(8,128)(2,1)}, bf16[256,768]{1,0:T(8,128)(2,1)}, u32[]{:S(2)}, u32[]{:S(2)}) collective-permute-start(bf16[256,768]{1,0:T(8,128)(2,1)} %bitcast.57), channel_id=1, source_target_pairs={{0,3},{1,0},{2,1},{3,2},{4,7},{5,4},{6,5},{7,6},{8,11},{9,8},{10,9... | collective-permute-start | bytes 1179656 | tf_op jit(solution)/shard_map/ppermute | solution.py:586
  14.5 94.0 %collective-permute-start.1 = (bf16[256,768]{1,0:T(8,128)(2,1)}, bf16[256,768]{1,0:T(8,128)(2,1)}, u32[]{:S(2)}, u32[]{:S(2)}) collective-permute-start(bf16[256,768]{1,0:T(8,128)(2,1)} %bitcast.58), channel_id=1, source_target_pairs={{0,2},{1,3},{2,0},{3,1},{4,6},{5,7},{6,4},{7,5},{8,10},{9,11},{10,... | collective-permute-start | bytes 1179656 | tf_op jit(solution)/shard_map/ppermute | solution.py:586
  15.8 92.6 %collective-permute-start = (bf16[256,768]{1,0:T(8,128)(2,1)}, bf16[256,768]{1,0:T(8,128)(2,1)}, u32[]{:S(2)}, u32[]{:S(2)}) collective-permute-start(bf16[256,768]{1,0:T(8,128)(2,1)} %bitcast.59), channel_id=1, source_target_pairs={{0,1},{1,2},{2,3},{3,0},{4,5},{5,6},{6,7},{7,4},{8,9},{9,10},{10,1... | collective-permute-start | bytes 1179656 | tf_op jit(solution)/shard_map/ppermute | solution.py:586
  20.5 1.6 %copy-start.6 = (bf16[16,8,1440]{2,1,0:T(8,128)(2,1)S(1)}, bf16[16,8,1440]{2,1,0:T(8,128)(2,1)}, u32[]{:S(2)}) copy-start(bf16[16,8,1440]{2,1,0:T(8,128)(2,1)} %param.17) | copy-start | bytes 1105924
  20.6 2.2 %copy-start.3 = (f32[256,1440]{0,1:T(8,128)S(1)}, f32[256,1440]{0,1:T(8,128)}, u32[]{:S(2)}) copy-start(f32[256,1440]{0,1:T(8,128)} %constant.88.clone) | copy-start | bytes 4423684
  20.6 2.5 %copy-start.4 = (f32[16,8,1440]{2,1,0:T(8,128)S(1)}, f32[16,8,1440]{2,1,0:T(8,128)}, u32[]{:S(2)}) copy-start(f32[16,8,1440]{2,1,0:T(8,128)} %param.18) | copy-start | bytes 2211844
  86.7 4.4 %copy-start.8 = (f32[1536]{0:T(1024)S(1)}, f32[1536]{0:T(1024)}, u32[]{:S(2)}) copy-start(f32[1536]{0:T(1024)} %param.15) | copy-start | bytes 18436
  92.4 2.8 %copy-start = (bf16[1536,3,4,96]{0,3,2,1:T(8,128)(2,1)S(1)}, bf16[1536,3,4,96]{0,3,2,1:T(8,128)(2,1)}, u32[]{:S(2)}) copy-start(bf16[1536,3,4,96]{0,3,2,1:T(8,128)(2,1)} %param.13) | copy-start | bytes 10616836
  98.9 6.1 %copy-start.7 = (bf16[4,720,256]{2,1,0:T(8,128)(2,1)S(1)}, bf16[4,720,256]{2,1,0:T(8,128)(2,1)}, u32[]{:S(2)}) copy-start(bf16[4,720,256]{2,1,0:T(8,128)(2,1)} %constant.91) | copy-start | bytes 4423684
  99.0 7.1 %copy-start.2 = (f32[256,1440,1]{0,1,2:T(8,128)S(1)}, f32[256,1440,1]{0,1,2:T(8,128)}, u32[]{:S(2)}) copy-start(f32[256,1440,1]{0,1,2:T(8,128)} %constant.92) | copy-start | bytes 4423684
  99.0 7.1 %copy-start.5 = (f32[256,128]{0,1:T(8,128)S(1)}, f32[256,128]{0,1:T(8,128)}, u32[]{:S(2)}) copy-start(f32[256,128]{0,1:T(8,128)} %reshape.118) | copy-start | bytes 393220
  105.0 3.5 %copy-start.1 = (bf16[256,1,768]{2,0,1:T(8,128)(2,1)S(1)}, bf16[256,1,768]{2,0,1:T(8,128)(2,1)}, u32[]{:S(2)}) copy-start(bf16[256,1,768]{2,0,1:T(8,128)(2,1)} %copy.43) | copy-start | bytes 1179652
